TPU v7x, 128 devices: a whole 4x4x4 slice. The times are simulated.
128 devices in a mesh: dp: 8 (over y, core), expert: 16 (over x, z).
Axes of the slice: x: 4, y: 4, z: 4, core: 2. Of those that a mesh axis runs over, the one named last changes fastest.
Arguments:
- tokens: bfloat16 [8192, 2048], P(('dp', 'expert')), may hold values from -6 to 6
- grad_out: bfloat16 [8192, 2048], P(('dp', 'expert')), may hold values from -6 to 6
- probs: float32 [8192, 128], P(('dp', 'expert')), may hold values from 0.01 to 1
- expert_ids: int32 [8192, 8], P(('dp', 'expert')), may hold values from 0 to 127, all different within a row; in each aligned block of 64 rows (0 to 63, 64 to 127, ...) at most 8 rows name the same one
- w_gate: bfloat16 [128, 2048, 768], P(('dp', 'expert')), may hold values from -0.125 to 0.125
- w_up: bfloat16 [128, 2048, 768], P(('dp', 'expert')), may hold values from -0.125 to 0.125
- w_down: bfloat16 [128, 768, 2048], P(('dp', 'expert')), may hold values from -0.21875 to 0.21875
Outputs:
- d_tokens: bfloat16 [8192, 2048], P(('dp', 'expert'))
- d_probs: float32 [8192, 128], P(('dp', 'expert'))
- d_gate: bfloat16 [128, 2048, 768], P(('dp', 'expert'))
- d_up: bfloat16 [128, 2048, 768], P(('dp', 'expert'))
- d_down: bfloat16 [128, 768, 2048], P(('dp', 'expert'))
Inputs may be any that keep to these rules, and one draw needn't show every extreme that they name: `expert_ids`: each token names 8 different experts. In the 64 tokens of one device no expert is named more than 8 times, and in every draw some expert is named exactly 8 times by the tokens of some device.
All inputs are finite; a program needn't handle non-finite values.
Results may differ from a plain program's by a relative error of at most 0.014.
Values may be sent and summed in bfloat16 or wider, within the bound.
No kernel may reach another device: no remote copies, remote signals or barrier semaphores. Data moves between devices by JAX's collectives and lax.ppermute only.
A program may use at most 128 MiB of HBM per device.

v0:
```python
import jax
import jax.numpy as jnp
from jax import lax
from jax.experimental import pallas as pl
from jax.experimental.pallas import tpu as pltpu
from jax.sharding import PartitionSpec as P

aux_weight = 1.0
CAP = 8
LANES = 128
AXES = ("dp", "expert")
f32 = jnp.float32
bf16 = jnp.bfloat16


def iota(shape, dim):
    return lax.broadcasted_iota(jnp.int32, shape, dim)


def nn(left, right):
    return jnp.dot(left, right, preferred_element_type=f32)


def nt(left, right):
    return lax.dot_general(left, right, (((1,), (1,)), ((), ())), preferred_element_type=f32)


def tn(left, right):
    return lax.dot_general(left, right, (((0,), (0,)), ((), ())), preferred_element_type=f32)


def send_kernel(ids_ref, probs_ref, tok_ref, grad_ref, x_ref, pick_ref, w_ref, sum_ref, cnt_ref, rank_s, w_s):
    step = pl.program_id(0)
    rows = x_ref.shape[0]
    toks, experts = probs_ref.shape
    width = tok_ref.shape[1]

    @pl.when(step == 0)
    def _():
        lane = iota((toks, experts), 1)
        member = jnp.zeros((toks, experts), jnp.bool_)
        for k in range(ids_ref.shape[1]):
            member = jnp.logical_or(member, ids_ref[:, k : k + 1] == lane)
        named = member.astype(f32)
        picked = jnp.where(member, probs_ref[...], 0.0)
        total = jnp.sum(picked, axis=1, keepdims=True)
        weight = (picked / total).astype(bf16)
        before = (iota((toks, toks), 0) > iota((toks, toks), 1)).astype(bf16)
        rank = nn(before, named.astype(bf16))
        rank = jnp.where(member, rank, 100.0).astype(bf16)
        rank_s[...] = rank
        w_s[...] = weight
        w_ref[...] = weight.astype(f32)
        sum_ref[...] = jnp.broadcast_to(total, sum_ref.shape)
        count = jnp.sum(named, axis=0, keepdims=True)
        mine = iota(cnt_ref.shape, 0) % CAP == iota(cnt_ref.shape, 1) // (LANES // CAP)
        cnt_ref[...] = jnp.where(mine, jnp.broadcast_to(count, cnt_ref.shape), 0.0)
        slots = pick_ref.shape[1]
        spread_t = (iota((experts, slots), 0) == iota((experts, slots), 1) // CAP).astype(bf16)
        rank_all = nn(rank, spread_t)
        pick_ref[...] = (rank_all == (iota((toks, slots), 1) % CAP).astype(f32)).astype(bf16)

    spread = ((iota((rows, experts), 0) + step * rows) // CAP == iota((rows, experts), 1)).astype(bf16)
    chosen = nt(spread, rank_s[...]) == (iota((rows, toks), 0) % CAP).astype(f32)
    weights = nt(spread, w_s[...])
    x_ref[:, :width] = nn(chosen.astype(bf16), tok_ref[...]).astype(bf16)
    x_ref[:, width:] = nn(jnp.where(chosen, weights, 0.0).astype(bf16), grad_ref[...]).astype(bf16)


def send_rows(ids, probs, tokens, grads):
    toks, width = tokens.shape
    experts = probs.shape[1]
    slots = experts * CAP
    rows = 256
    whole = lambda shape: pl.BlockSpec(shape, lambda i: (0, 0))
    return pl.pallas_call(
        send_kernel,
        grid=(slots // rows,),
        in_specs=[whole(ids.shape), whole(probs.shape), whole(tokens.shape), whole(grads.shape)],
        out_specs=[
            pl.BlockSpec((rows, 2 * width), lambda i: (i, 0)),
            whole((toks, slots)),
            whole((toks, experts)),
            whole((toks, experts)),
            whole((rows, LANES)),
        ],
        out_shape=[
            jax.ShapeDtypeStruct((slots, 2 * width), bf16),
            jax.ShapeDtypeStruct((toks, slots), bf16),
            jax.ShapeDtypeStruct((toks, experts), f32),
            jax.ShapeDtypeStruct((toks, experts), f32),
            jax.ShapeDtypeStruct((rows, LANES), f32),
        ],
        scratch_shapes=[pltpu.VMEM((toks, experts), bf16), pltpu.VMEM((toks, experts), bf16)],
        compiler_params=pltpu.CompilerParams(vmem_limit_bytes=24 << 20),
        name="send_rows",
    )(ids, probs, tokens, grads)


def expert_kernel(tok_ref, grad_ref, gate_ref, up_ref, down_ref, cnt_ref, out_ref, hid_ref, dg_ref, du_ref):
    rows, width = tok_ref.shape
    tok = tok_ref[...]
    gate = nn(tok, gate_ref[...])
    up = nn(tok, up_ref[...])
    back = nt(grad_ref[...], down_ref[...])
    sig = jax.nn.sigmoid(gate)
    silu = gate * sig
    hidden = (silu * up).astype(bf16)
    hid_ref[...] = hidden
    route = jnp.sum(hidden.astype(f32) * back, axis=1, keepdims=True)
    d_gate = (back * up * sig * (1.0 + gate * (1.0 - sig))).astype(bf16)
    d_up = (back * silu).astype(bf16)
    dg_ref[...] = d_gate
    du_ref[...] = d_up
    out_ref[:, :width] = (nt(d_gate, gate_ref[...]) + nt(d_up, up_ref[...])).astype(bf16)
    high = route.astype(bf16).astype(f32)
    turn = (iota((rows, LANES), 1) // (LANES // CAP) - iota((rows, LANES), 0) % CAP + CAP) % CAP
    extra = jnp.where(turn == 4, high, jnp.where(turn == 5, route - high, cnt_ref[...]))
    out_ref[:, width:] = extra.astype(bf16)


def expert_rows(x, gate, up, down, counts):
    slots = x.shape[0]
    width, units = gate.shape
    rows = counts.shape[0]
    whole = lambda shape: pl.BlockSpec(shape, lambda i: (0, 0), pipeline_mode=pl.Buffered(1))
    block = lambda cols, at: pl.BlockSpec((rows, cols), lambda i: (i, at))
    part = jax.ShapeDtypeStruct((slots, units), bf16)
    return pl.pallas_call(
        expert_kernel,
        grid=(slots // rows,),
        in_specs=[
            block(width, 0),
            block(width, 1),
            whole(gate.shape),
            whole(up.shape),
            whole(down.shape),
            whole(counts.shape),
        ],
        out_specs=[block(width + LANES, 0), block(units, 0), block(units, 0), block(units, 0)],
        out_shape=[jax.ShapeDtypeStruct((slots, width + LANES), bf16), part, part, part],
        compiler_params=pltpu.CompilerParams(vmem_limit_bytes=48 << 20),
        name="expert_rows",
    )(x, x, gate, up, down, counts)


def tail_kernel(scale, pick_ref, back_ref, extra_ref, w_ref, sum_ref, tok_ref, prob_ref, acc, route_s, load_s):
    step = pl.program_id(0)
    rows = back_ref.shape[0]
    experts = w_ref.shape[1]

    @pl.when(step == 0)
    def _():
        acc[...] = jnp.zeros_like(acc)
        route_s[...] = jnp.zeros_like(route_s)
        load_s[...] = jnp.zeros_like(load_s)

    pick = pick_ref[...]
    acc[...] += nn(pick, back_ref[...])
    extra = extra_ref[...].astype(f32)
    turn = (iota((rows, LANES), 1) // (LANES // CAP) - iota((rows, LANES), 0) % CAP + CAP) % CAP
    first = iota((rows, LANES), 1) % (LANES // CAP) == 0
    high = jnp.sum(jnp.where(jnp.logical_and(first, turn == 4), extra, 0.0), axis=1, keepdims=True)
    low = jnp.sum(jnp.where(jnp.logical_and(first, turn == 5), extra, 0.0), axis=1, keepdims=True)
    own = (iota((rows, experts), 0) + step * rows) // CAP == iota((rows, experts), 1)
    route_s[...] += nn(pick, jnp.where(own, high, 0.0).astype(bf16)) + nn(
        pick, jnp.where(own, low, 0.0).astype(bf16)
    )
    load_s[...] += jnp.sum(jnp.where(turn == 0, extra, 0.0), axis=0, keepdims=True)

    @pl.when(step == pl.num_programs(0) - 1)
    def _():
        tok_ref[...] = acc[...].astype(bf16)
        weight = w_ref[...]
        named = weight > 0.0
        total = sum_ref[...]
        route = jnp.where(named, route_s[...] / jnp.where(named, weight, 1.0), 0.0)
        route = route.astype(bf16).astype(f32)
        mean = jnp.sum(route * weight, axis=1, keepdims=True)
        prob_ref[...] = jnp.where(named, (route - mean) / total, 0.0) + load_s[...] * scale


def collect_rows(scale, pick, back, weight, total):
    toks, slots = pick.shape
    experts = weight.shape[1]
    width = back.shape[1] - LANES
    rows = 256
    whole = lambda shape: pl.BlockSpec(shape, lambda i: (0, 0))
    return pl.pallas_call(
        lambda *refs: tail_kernel(scale, *refs),
        grid=(slots // rows,),
        in_specs=[
            pl.BlockSpec((toks, rows), lambda i: (0, i)),
            pl.BlockSpec((rows, width), lambda i: (i, 0)),
            pl.BlockSpec((rows, LANES), lambda i: (i, width // LANES)),
            whole(weight.shape),
            whole(total.shape),
        ],
        out_specs=[whole((toks, width)), whole((toks, experts))],
        out_shape=[jax.ShapeDtypeStruct((toks, width), bf16), jax.ShapeDtypeStruct((toks, experts), f32)],
        scratch_shapes=[
            pltpu.VMEM((toks, width), f32),
            pltpu.VMEM((toks, experts), f32),
            pltpu.VMEM((1, LANES), f32),
        ],
        compiler_params=pltpu.CompilerParams(vmem_limit_bytes=24 << 20),
        name="collect_rows",
    )(pick, back, back, weight, total)


def exchange(rows, devices):
    slots, width = rows.shape
    moved = lax.all_to_all(
        rows.reshape(devices, slots // devices, width), AXES, split_axis=0, concat_axis=0, tiled=True
    )
    return moved.reshape(slots, width)


def on_device(tokens, grad_out, probs, expert_ids, w_gate, w_up, w_down):
    toks, width = tokens.shape
    experts = probs.shape[1]
    devices = lax.axis_size("dp") * lax.axis_size("expert")
    x, pick, weight, total, counts = send_rows(expert_ids, probs, tokens, grad_out)
    x = exchange(x, devices)
    out, hidden, d_gate_pre, d_up_pre = expert_rows(x, w_gate[0], w_up[0], w_down[0], counts)
    back = exchange(out, devices)
    d_gate = tn(x[:, :width], d_gate_pre).astype(bf16)
    d_up = tn(x[:, :width], d_up_pre).astype(bf16)
    d_down = tn(hidden, x[:, width:]).astype(bf16)
    scale = aux_weight * experts / (devices * toks * expert_ids.shape[1])
    d_tokens, d_probs = collect_rows(scale, pick, back, weight, total)
    return (d_tokens, d_probs, d_gate[None], d_up[None], d_down[None])


def solution(mesh):
    flat = P(AXES, None)
    deep = P(AXES, None, None)
    return jax.shard_map(
        on_device,
        mesh=mesh,
        in_specs=(flat, flat, flat, flat, deep, deep, deep),
        out_specs=(flat, flat, deep, deep, deep),
        check_vma=False,
    )
```

profile of v0, /device:TPU:1, one launch (start us, length us, event | category | flops | bytes accessed | tf_op | source)
XLA Modules:
  0.0 208.5 jit_solution(1173083929877913377)
XLA Ops:
  0.6 0.8 copy.12.ids_ref
  1.4 0.0 copy-start
  1.4 0.9 copy-done
  2.4 0.0 copy-start.1
  2.4 0.9 copy-done.1
  3.3 0.0 copy-start.2
  3.3 0.8 copy-done.2
  4.1 3.8 %send_rows.1 = (bf16[1024,4096]{1,0:T(8,128)(2,1)S(1)}, bf16[64,1024]{1,0:T(8,128)(2,1)S(1)}, f32[64,128]{1,0:T(8,128)S(1)}, f32[64,128]{1,0:T(8,128)S(1)}, f32[256,128]{1,0:T(8,128)S(1)}) custom-call(s32[64,8]{1,0:T(8,128)S(1)} %copy.12.ids_ref, f32[64,128]{1,0:T(8,128)S(1)} %copy-done.2, bf16[64,2048]{1,0:T(8,128)(2,1)S(1)} %copy-done, ...), custom_call_target="tpu_custom_call" | custom-call | tf_op jit(solution)/shard_map/send_rows/pallas_call | solution.py:76
  7.8 108.8 %all_to_all.10 = bf16[128,8,4096]{2,1,0:T(8,128)(2,1)} all-to-all(bf16[128,8,4096]{2,1,0:T(8,128)(2,1)S(1)} %bitcast.16), channel_id=1, replica_groups=mesh['dp'=8,'expert'=16] {'dp','expert'}, dimensions={0} | all-to-all | bytes 16777216 | tf_op jit(solution)/shard_map/all_to_all | solution.py:213
  116.6 25.8 %expert_rows.1 = (bf16[1024,2176]{1,0:T(8,128)(2,1)}, bf16[1024,768]{1,0:T(8,128)(2,1)S(1)}, bf16[1024,768]{1,0:T(8,128)(2,1)S(1)}, bf16[1024,768]{1,0:T(8,128)(2,1)S(1)}) custom-call(bf16[1024,4096]{1,0:T(8,128)(2,1)} %bitcast.17, bf16[1024,4096]{1,0:T(8,128)(2,1)} %bitcast.18, bf16[2048,768]{1,0:T(8,128)(2,1)} %bitcast.25, bf16[2048,768]{1,0:T(8,128)(2,1)} %bitcast.26, ...), custom_call_target="tpu_custom_call" | custom-call | tf_op jit(solution)/shard_map/expert_rows/pallas_call | solution.py:129
  142.4 0.0 copy-start.3
  142.4 1.1 copy-done.3
  143.6 5.0 %all-to-all-start.1 = ((bf16[128,8,2176]{2,1,0:T(8,128)(2,1)}), bf16[128,8,2176]{2,1,0:T(8,128)(2,1)}, u32[]{:S(2)}, u32[]{:S(2)}) async-start(bf16[128,8,2176]{2,1,0:T(8,128)(2,1)} %bitcast.24), calls=%async_computation.1 | async-start | bytes 8912896 | tf_op jit(solution)/shard_map/all_to_all | solution.py:213
  148.6 0.0 slice-start
  148.6 8.0 %fusion.21 = bf16[1,2048,768]{2,1,0:T(8,128)(2,1)} fusion(bf16[1024,768]{1,0:T(8,128)(2,1)} %copy-done.3, bf16[1024,4096]{1,0:T(8,128)(2,1)} %bitcast.19), kind=kOutput, calls=%fused_computation.11 | convolution fusion | flops 3222798336 | bytes 8912896 | tf_op jit(solution)/shard_map/dot_general | solution.py:29
  156.7 0.0 slice-start.1
  156.7 7.5 %fusion.18 = bf16[1,2048,768]{2,1,0:T(8,128)(2,1)} fusion(bf16[1024,768]{1,0:T(8,128)(2,1)S(1)} %get-tuple-element.25, bf16[1024,4096]{1,0:T(8,128)(2,1)} %bitcast.20), kind=kOutput, calls=%fused_computation.10 | convolution fusion | flops 3222798336 | bytes 8912896 | tf_op jit(solution)/shard_map/dot_general | solution.py:29
  164.2 0.0 slice-done
  164.2 0.0 slice-done.1
  164.2 4.8 %fusion.15 = bf16[1,768,2048]{2,1,0:T(8,128)(2,1)} fusion(bf16[1024,768]{1,0:T(8,128)(2,1)S(1)} %get-tuple-element.26, bf16[1024,4096]{1,0:T(8,128)(2,1)S(1)} %bitcast.23), kind=kOutput, calls=%fused_computation.9 | convolution fusion | flops 3222798336 | bytes 8912896 | tf_op jit(solution)/shard_map/dot_general | solution.py:29
  169.0 34.7 %all-to-all-done.1 = bf16[128,8,2176]{2,1,0:T(8,128)(2,1)} async-done(((bf16[128,8,2176]{2,1,0:T(8,128)(2,1)}), bf16[128,8,2176]{2,1,0:T(8,128)(2,1)}, u32[]{:S(2)}, u32[]{:S(2)}) %all-to-all-start.1) | async-done | bytes 4456480 | tf_op jit(solution)/shard_map/all_to_all | solution.py:213
  203.7 4.7 %collect_rows.1 = (bf16[64,2048]{1,0:T(8,128)(2,1)}, f32[64,128]{1,0:T(8,128)}) custom-call(bf16[64,1024]{1,0:T(8,128)(2,1)S(1)} %get-tuple-element.16.refs_0_, bf16[1024,2176]{1,0:T(8,128)(2,1)} %bitcast.6.refs_1_.refs_2_, bf16[1024,2176]{1,0:T(8,128)(2,1)} %bitcast.6.refs_1_.refs_2_, f32[64,128]{1,0:T(8,128)S(1)} %get-tuple-element.20.refs_3_, ...), custom_call_target="tpu_custom_call" | custom-call | tf_op jit(solution)/shard_map/collect_rows/pallas_call | solution.py:189
  (1 shorter events, 0.0 us)
Async XLA Ops:
  1.4 0.9 copy-start
  2.4 0.9 copy-start.1
  3.3 0.8 copy-start.2
  142.4 1.1 copy-start.3
  143.6 60.2 %all-to-all-start.1 = ((bf16[128,8,2176]{2,1,0:T(8,128)(2,1)}), bf16[128,8,2176]{2,1,0:T(8,128)(2,1)}, u32[]{:S(2)}, u32[]{:S(2)}) async-start(bf16[128,8,2176]{2,1,0:T(8,128)(2,1)} %bitcast.24), calls=%async_computation.1 | async-start | bytes 8912896 | tf_op jit(solution)/shard_map/all_to_all | solution.py:213
  148.6 15.6 %slice-start = ((s8[8388608]{0:T(1024)(128)(4,1)}), s8[4194304]{0:T(1024)(128)(4,1)S(1)}, s32[]{:S(2)}) async-start(s8[8388608]{0:T(1024)(128)(4,1)} %bitcast.21), calls=%async_computation.2 | async-start | bytes 8388608
  156.7 7.5 %slice-start.1 = ((s8[8388608]{0:T(1024)(128)(4,1)}), s8[4194304]{0:T(1024)(128)(4,1)S(1)}, s32[]{:S(2)}) async-start(s8[8388608]{0:T(1024)(128)(4,1)} %bitcast.21), calls=%async_computation.3 | async-start | bytes 8388608
where the time goes:
time: 209 us; the launch traced here: 208 us
  blocking collectives  109 us (52%)
  waiting for transfers between devices  34.7 us (17%)
  Pallas kernels  34.3 us (16%)
  matrix products  20.4 us (10%)
  starting transfers between devices  5.05 us (2%)
  local copies, waits for them, and re-layouts  4.58 us (2%)
    all_to_all x1, blocking collectives, exchange(): lax.all_to_all(rows.reshape(devices, slots // devices, width), AXES, spli...  109 us
    all_to_all x1, waiting for transfers between devices, exchange(): lax.all_to_all(rows.reshape(devices, slots // devices, width), AXES, spli...  34.7 us
    pallas_call x1, Pallas kernels, expert_rows(): pl.pallas_call(expert_kernel, grid=(slots // rows,), in_specs=[block(widt...  25.8 us
    dot_general x3, matrix products, tn(): lax.dot_general(left, right, (((0,), (0,)), ((), ())), preferred_element_...  20.4 us
    all_to_all x1, starting transfers between devices, exchange(): lax.all_to_all(rows.reshape(devices, slots // devices, width), AXES, spli...  5.05 us
    pallas_call x1, Pallas kernels, collect_rows(): pl.pallas_call(lambda *refs: tail_kernel(scale, *refs), grid=(slots // ro...  4.74 us
    unnamed x13, local copies, waits for them, and re-layouts  4.58 us
  transfers between devices with their start and end apart: 1, of which 1 were waited for; matrix products, arithmetic and copies ran while one was open for 10% of the time, Pallas kernels for 0%

commit v1 on v0

--- a/solution.py
+++ b/solution.py
@@ -29,6 +29,14 @@
     return lax.dot_general(left, right, (((0,), (0,)), ((), ())), preferred_element_type=f32)
 
 
+def in_hbm(array):
+    return pltpu.with_memory_space_constraint(array, pltpu.HBM)
+
+
+def in_vmem(array):
+    return pltpu.with_memory_space_constraint(array, pltpu.VMEM)
+
+
 def send_kernel(ids_ref, probs_ref, tok_ref, grad_ref, x_ref, pick_ref, w_ref, sum_ref, cnt_ref, rank_s, w_s):
     step = pl.program_id(0)
     rows = x_ref.shape[0]
@@ -37,11 +45,13 @@
 
     @pl.when(step == 0)
     def _():
-        lane = iota((toks, experts), 1)
-        member = jnp.zeros((toks, experts), jnp.bool_)
-        for k in range(ids_ref.shape[1]):
-            member = jnp.logical_or(member, ids_ref[:, k : k + 1] == lane)
-        named = member.astype(f32)
+        expert = iota((experts, toks), 0)
+        member_t = ids_ref[0:1, :] == expert
+        for k in range(1, ids_ref.shape[0]):
+            member_t = jnp.logical_or(member_t, ids_ref[k : k + 1, :] == expert)
+        same = (iota((experts, experts), 0) == iota((experts, experts), 1)).astype(bf16)
+        named = tn(member_t.astype(f32).astype(bf16), same)
+        member = named > 0.5
         picked = jnp.where(member, probs_ref[...], 0.0)
         total = jnp.sum(picked, axis=1, keepdims=True)
         weight = (picked / total).astype(bf16)
@@ -73,6 +83,7 @@
     slots = experts * CAP
     rows = 256
     whole = lambda shape: pl.BlockSpec(shape, lambda i: (0, 0))
+    ids, probs, tokens, grads = [in_hbm(a) for a in (ids.T, probs, tokens, grads)]
     return pl.pallas_call(
         send_kernel,
         grid=(slots // rows,),
@@ -112,7 +123,9 @@
     d_up = (back * silu).astype(bf16)
     dg_ref[...] = d_gate
     du_ref[...] = d_up
-    out_ref[:, :width] = (nt(d_gate, gate_ref[...]) + nt(d_up, up_ref[...])).astype(bf16)
+    for at in range(0, width, 512):
+        cols = slice(at, at + 512)
+        out_ref[:, cols] = (nt(d_gate, gate_ref[cols, :]) + nt(d_up, up_ref[cols, :])).astype(bf16)
     high = route.astype(bf16).astype(f32)
     turn = (iota((rows, LANES), 1) // (LANES // CAP) - iota((rows, LANES), 0) % CAP + CAP) % CAP
     extra = jnp.where(turn == 4, high, jnp.where(turn == 5, route - high, cnt_ref[...]))
@@ -139,7 +152,7 @@
         ],
         out_specs=[block(width + LANES, 0), block(units, 0), block(units, 0), block(units, 0)],
         out_shape=[jax.ShapeDtypeStruct((slots, width + LANES), bf16), part, part, part],
-        compiler_params=pltpu.CompilerParams(vmem_limit_bytes=48 << 20),
+        compiler_params=pltpu.CompilerParams(vmem_limit_bytes=50 << 20),
         name="expert_rows",
     )(x, x, gate, up, down, counts)
 
@@ -222,7 +235,8 @@
     devices = lax.axis_size("dp") * lax.axis_size("expert")
     x, pick, weight, total, counts = send_rows(expert_ids, probs, tokens, grad_out)
     x = exchange(x, devices)
-    out, hidden, d_gate_pre, d_up_pre = expert_rows(x, w_gate[0], w_up[0], w_down[0], counts)
+    gate, up, down = [in_vmem(w[0]) for w in (w_gate, w_up, w_down)]
+    out, hidden, d_gate_pre, d_up_pre = expert_rows(x, gate, up, down, counts)
     back = exchange(out, devices)
     d_gate = tn(x[:, :width], d_gate_pre).astype(bf16)
     d_up = tn(x[:, :width], d_up_pre).astype(bf16)

time: 209 us -> 200 us (0.957)
  local copies, waits for them, and re-layouts: 4.58 us -> 0.05 us
  Pallas kernels: 34.3 us -> 30.3 us
    pallas_call x1, Pallas kernels: 25.8 us -> 20.7 us  [expert_rows(): pl.pallas_call(expert_kernel, grid=(slots // rows,), in_specs=[block(widt...]
    unnamed x13 -> x18, local copies, waits for them, and re-layouts: 4.58 us -> 0.05 us
where the time goes in v1:
time: 200 us
  blocking collectives  109 us (54%)
  waiting for transfers between devices  35.1 us (18%)
  Pallas kernels  30.3 us (15%)
  matrix products  19.9 us (10%)
  starting transfers between devices  5.18 us (3%)
    all_to_all x1, blocking collectives, exchange(): lax.all_to_all(rows.reshape(devices, slots // devices, width), AXES, spli...  109 us
    all_to_all x1, waiting for transfers between devices, exchange(): lax.all_to_all(rows.reshape(devices, slots // devices, width), AXES, spli...  35.1 us
    pallas_call x1, Pallas kernels, expert_rows(): pl.pallas_call(expert_kernel, grid=(slots // rows,), in_specs=[block(widt...  20.7 us
    dot_general x3, matrix products, tn(): lax.dot_general(left, right, (((0,), (0,)), ((), ())), preferred_element_...  19.9 us
    all_to_all x1, starting transfers between devices, exchange(): lax.all_to_all(rows.reshape(devices, slots // devices, width), AXES, spli...  5.18 us
    pallas_call x1, Pallas kernels, send_rows(): pl.pallas_call(send_kernel, grid=(slots // rows,), in_specs=[whole(ids.sh...  4.93 us
    pallas_call x1, Pallas kernels, collect_rows(): pl.pallas_call(lambda *refs: tail_kernel(scale, *refs), grid=(slots // ro...  4.74 us
  transfers between devices with their start and end apart: 1, of which 1 were waited for; matrix products, arithmetic and copies ran while one was open for 10% of the time, Pallas kernels for 0%

profile of v1, /device:TPU:1, one launch (start us, length us, event | category | flops | bytes accessed | tf_op | source)
XLA Modules:
  0.0 200.2 jit_solution(13481067239847372119)
XLA Ops:
  0.6 4.9 %send_rows.1 = (bf16[1024,4096]{1,0:T(8,128)(2,1)S(1)}, bf16[64,1024]{1,0:T(8,128)(2,1)S(1)}, f32[64,128]{1,0:T(8,128)S(1)}, f32[64,128]{1,0:T(8,128)S(1)}, f32[256,128]{1,0:T(8,128)S(1)}) custom-call(s32[8,64]{1,0:T(8,128)} %bitcast.29, f32[64,128]{1,0:T(8,128)} %probs_ref.1, bf16[64,2048]{1,0:T(8,128)(2,1)} %tok_ref.1, bf16[64,2048]{1,0:T(8,128)(2,1)} %grad_ref.1), custom_call_target="tpu_custom_call" | custom-call | tf_op jit(solution)/shard_map/send_rows/pallas_call | solution.py:87
  5.6 0.0 copy-start.3
  5.6 0.0 copy-start
  5.6 0.0 copy-start.1
  5.6 0.0 copy-start.2
  5.6 108.8 %all_to_all.10 = bf16[128,8,4096]{2,1,0:T(8,128)(2,1)} all-to-all(bf16[128,8,4096]{2,1,0:T(8,128)(2,1)S(1)} %bitcast.17), channel_id=1, replica_groups=mesh['dp'=8,'expert'=16] {'dp','expert'}, dimensions={0} | all-to-all | bytes 16777216 | tf_op jit(solution)/shard_map/all_to_all | solution.py:226
  114.4 0.0 copy-done.3
  114.4 0.0 copy-done
  114.4 0.0 copy-done.1
  114.4 0.0 copy-done.2
  114.5 20.7 %expert_rows.1 = (bf16[1024,2176]{1,0:T(8,128)(2,1)}, bf16[1024,768]{1,0:T(8,128)(2,1)}, bf16[1024,768]{1,0:T(8,128)(2,1)}, bf16[1024,768]{1,0:T(8,128)(2,1)}) custom-call(bf16[1024,4096]{1,0:T(8,128)(2,1)} %bitcast.21, bf16[1024,4096]{1,0:T(8,128)(2,1)} %bitcast.22, bf16[2048,768]{1,0:T(8,128)(2,1)S(1)} %bitcast.18, bf16[2048,768]{1,0:T(8,128)(2,1)S(1)} %bitcast.19, ...), custom_call_target="tpu_custom_call" | custom-call | tf_op jit(solution)/shard_map/expert_rows/pallas_call | solution.py:142
  135.1 0.0 copy-start.6
  135.1 5.2 %all-to-all-start.1 = ((bf16[128,8,2176]{2,1,0:T(8,128)(2,1)}), bf16[128,8,2176]{2,1,0:T(8,128)(2,1)}, u32[]{:S(2)}, u32[]{:S(2)}) async-start(bf16[128,8,2176]{2,1,0:T(8,128)(2,1)} %bitcast.28), calls=%async_computation.1 | async-start | bytes 8912896 | tf_op jit(solution)/shard_map/all_to_all | solution.py:226
  140.3 0.0 copy-done.6
  140.3 0.0 copy-start.5
  140.3 0.0 slice-start
  140.3 7.5 %fusion.21 = bf16[1,2048,768]{2,1,0:T(8,128)(2,1)} fusion(bf16[1024,768]{1,0:T(8,128)(2,1)S(1)} %copy-done.6, bf16[1024,4096]{1,0:T(8,128)(2,1)} %bitcast.23), kind=kOutput, calls=%fused_computation.11 | convolution fusion | flops 3222798336 | bytes 8912896 | tf_op jit(solution)/shard_map/dot_general | solution.py:29
  147.9 0.0 copy-done.5
  147.9 0.0 slice-start.1
  147.9 0.0 copy-start.4
  147.9 7.6 %fusion.18 = bf16[1,2048,768]{2,1,0:T(8,128)(2,1)} fusion(bf16[1024,768]{1,0:T(8,128)(2,1)S(1)} %copy-done.5, bf16[1024,4096]{1,0:T(8,128)(2,1)} %bitcast.24), kind=kOutput, calls=%fused_computation.10 | convolution fusion | flops 3222798336 | bytes 8912896 | tf_op jit(solution)/shard_map/dot_general | solution.py:29
  155.5 0.0 slice-done
  155.5 0.0 slice-done.1
  155.5 0.0 copy-done.4
  155.5 4.9 %fusion.15 = bf16[1,768,2048]{2,1,0:T(8,128)(2,1)} fusion(bf16[1024,768]{1,0:T(8,128)(2,1)S(1)} %copy-done.4, bf16[1024,4096]{1,0:T(8,128)(2,1)S(1)} %bitcast.27), kind=kOutput, calls=%fused_computation.9 | convolution fusion | flops 3222798336 | bytes 8912896 | tf_op jit(solution)/shard_map/dot_general | solution.py:29
  160.3 35.1 %all-to-all-done.1 = bf16[128,8,2176]{2,1,0:T(8,128)(2,1)} async-done(((bf16[128,8,2176]{2,1,0:T(8,128)(2,1)}), bf16[128,8,2176]{2,1,0:T(8,128)(2,1)}, u32[]{:S(2)}, u32[]{:S(2)}) %all-to-all-start.1) | async-done | bytes 4456480 | tf_op jit(solution)/shard_map/all_to_all | solution.py:226
  195.4 4.7 %collect_rows.1 = (bf16[64,2048]{1,0:T(8,128)(2,1)}, f32[64,128]{1,0:T(8,128)}) custom-call(bf16[64,1024]{1,0:T(8,128)(2,1)S(1)} %get-tuple-element.16.refs_0_, bf16[1024,2176]{1,0:T(8,128)(2,1)} %bitcast.7.refs_1_.refs_2_, bf16[1024,2176]{1,0:T(8,128)(2,1)} %bitcast.7.refs_1_.refs_2_, f32[64,128]{1,0:T(8,128)S(1)} %get-tuple-element.20.refs_3_, ...), custom_call_target="tpu_custom_call" | custom-call | tf_op jit(solution)/shard_map/collect_rows/pallas_call | solution.py:202
  (1 shorter events, 0.0 us)
Async XLA Ops:
  5.6 108.9 %copy-start.3 = (f32[256,128]{1,0:T(8,128)}, f32[256,128]{1,0:T(8,128)S(1)}, u32[]{:S(2)}) copy-start(f32[256,128]{1,0:T(8,128)S(1)} %get-tuple-element.18.cnt_ref) | copy-start | bytes 393220
  5.6 108.9 %copy-start = (bf16[1,2048,768]{2,1,0:T(8,128)(2,1)S(1)}, bf16[1,2048,768]{2,1,0:T(8,128)(2,1)}, u32[]{:S(2)}) copy-start(bf16[1,2048,768]{2,1,0:T(8,128)(2,1)} %param.11) | copy-start | bytes 9437188
  5.6 108.8 %copy-start.1 = (bf16[1,2048,768]{2,1,0:T(8,128)(2,1)S(1)}, bf16[1,2048,768]{2,1,0:T(8,128)(2,1)}, u32[]{:S(2)}) copy-start(bf16[1,2048,768]{2,1,0:T(8,128)(2,1)} %param.12) | copy-start | bytes 9437188
  5.6 108.8 %copy-start.2 = (bf16[1,768,2048]{2,1,0:T(8,128)(2,1)S(1)}, bf16[1,768,2048]{2,1,0:T(8,128)(2,1)}, u32[]{:S(2)}) copy-start(bf16[1,768,2048]{2,1,0:T(8,128)(2,1)} %param.13) | copy-start | bytes 9437188
  135.1 5.2 %copy-start.6 = (bf16[1024,768]{1,0:T(8,128)(2,1)S(1)}, bf16[1024,768]{1,0:T(8,128)(2,1)}, u32[]{:S(2)}) copy-start(bf16[1024,768]{1,0:T(8,128)(2,1)} %get-tuple-element.24) | copy-start | bytes 4718596
  135.1 60.3 %all-to-all-start.1 = ((bf16[128,8,2176]{2,1,0:T(8,128)(2,1)}), bf16[128,8,2176]{2,1,0:T(8,128)(2,1)}, u32[]{:S(2)}, u32[]{:S(2)}) async-start(bf16[128,8,2176]{2,1,0:T(8,128)(2,1)} %bitcast.28), calls=%async_computation.1 | async-start | bytes 8912896 | tf_op jit(solution)/shard_map/all_to_all | solution.py:226
  140.3 7.6 %copy-start.5 = (bf16[1024,768]{1,0:T(8,128)(2,1)S(1)}, bf16[1024,768]{1,0:T(8,128)(2,1)}, u32[]{:S(2)}) copy-start(bf16[1024,768]{1,0:T(8,128)(2,1)} %get-tuple-element.25) | copy-start | bytes 4718596
  140.3 15.1 %slice-start = ((s8[8388608]{0:T(1024)(128)(4,1)}), s8[4194304]{0:T(1024)(128)(4,1)S(1)}, s32[]{:S(2)}) async-start(s8[8388608]{0:T(1024)(128)(4,1)} %bitcast.25), calls=%async_computation.2 | async-start | bytes 8388608
  147.9 7.6 %slice-start.1 = ((s8[8388608]{0:T(1024)(128)(4,1)}), s8[4194304]{0:T(1024)(128)(4,1)S(1)}, s32[]{:S(2)}) async-start(s8[8388608]{0:T(1024)(128)(4,1)} %bitcast.25), calls=%async_computation.3 | async-start | bytes 8388608
  147.9 7.6 %copy-start.4 = (bf16[1024,768]{1,0:T(8,128)(2,1)S(1)}, bf16[1024,768]{1,0:T(8,128)(2,1)}, u32[]{:S(2)}) copy-start(bf16[1024,768]{1,0:T(8,128)(2,1)} %get-tuple-element.26) | copy-start | bytes 4718596

commit v2 on v1

--- a/solution.py
+++ b/solution.py
@@ -1,3 +1,5 @@
+import functools
+
 import jax
 import jax.numpy as jnp
 from jax import lax
@@ -9,6 +11,7 @@
 CAP = 8
 LANES = 128
 AXES = ("dp", "expert")
+ORDER = ("expert", "dp")
 f32 = jnp.float32
 bf16 = jnp.bfloat16
 
@@ -37,7 +40,12 @@
     return pltpu.with_memory_space_constraint(array, pltpu.VMEM)
 
 
-def send_kernel(ids_ref, probs_ref, tok_ref, grad_ref, x_ref, pick_ref, w_ref, sum_ref, cnt_ref, rank_s, w_s):
+def expert_of(slot, n_data, n_expert):
+    block = slot // CAP
+    return block % n_data * n_expert + block // n_data
+
+
+def send_kernel(sizes, ids_ref, probs_ref, tok_ref, grad_ref, x_ref, pick_ref, w_ref, sum_ref, cnt_ref, rank_s, w_s):
     step = pl.program_id(0)
     rows = x_ref.shape[0]
     toks, experts = probs_ref.shape
@@ -66,18 +74,19 @@
         mine = iota(cnt_ref.shape, 0) % CAP == iota(cnt_ref.shape, 1) // (LANES // CAP)
         cnt_ref[...] = jnp.where(mine, jnp.broadcast_to(count, cnt_ref.shape), 0.0)
         slots = pick_ref.shape[1]
-        spread_t = (iota((experts, slots), 0) == iota((experts, slots), 1) // CAP).astype(bf16)
+        spread_t = (iota((experts, slots), 0) == expert_of(iota((experts, slots), 1), *sizes)).astype(bf16)
         rank_all = nn(rank, spread_t)
         pick_ref[...] = (rank_all == (iota((toks, slots), 1) % CAP).astype(f32)).astype(bf16)
 
-    spread = ((iota((rows, experts), 0) + step * rows) // CAP == iota((rows, experts), 1)).astype(bf16)
+    slot = iota((rows, experts), 0) + step * rows
+    spread = (expert_of(slot, *sizes) == iota((rows, experts), 1)).astype(bf16)
     chosen = nt(spread, rank_s[...]) == (iota((rows, toks), 0) % CAP).astype(f32)
     weights = nt(spread, w_s[...])
     x_ref[:, :width] = nn(chosen.astype(bf16), tok_ref[...]).astype(bf16)
     x_ref[:, width:] = nn(jnp.where(chosen, weights, 0.0).astype(bf16), grad_ref[...]).astype(bf16)
 
 
-def send_rows(ids, probs, tokens, grads):
+def send_rows(sizes, ids, probs, tokens, grads):
     toks, width = tokens.shape
     experts = probs.shape[1]
     slots = experts * CAP
@@ -85,7 +94,7 @@
     whole = lambda shape: pl.BlockSpec(shape, lambda i: (0, 0))
     ids, probs, tokens, grads = [in_hbm(a) for a in (ids.T, probs, tokens, grads)]
     return pl.pallas_call(
-        send_kernel,
+        functools.partial(send_kernel, sizes),
         grid=(slots // rows,),
         in_specs=[whole(ids.shape), whole(probs.shape), whole(tokens.shape), whole(grads.shape)],
         out_specs=[
@@ -110,19 +119,22 @@
 
 def expert_kernel(tok_ref, grad_ref, gate_ref, up_ref, down_ref, cnt_ref, out_ref, hid_ref, dg_ref, du_ref):
     rows, width = tok_ref.shape
-    tok = tok_ref[...]
-    gate = nn(tok, gate_ref[...])
-    up = nn(tok, up_ref[...])
-    back = nt(grad_ref[...], down_ref[...])
-    sig = jax.nn.sigmoid(gate)
-    silu = gate * sig
-    hidden = (silu * up).astype(bf16)
-    hid_ref[...] = hidden
-    route = jnp.sum(hidden.astype(f32) * back, axis=1, keepdims=True)
-    d_gate = (back * up * sig * (1.0 + gate * (1.0 - sig))).astype(bf16)
-    d_up = (back * silu).astype(bf16)
-    dg_ref[...] = d_gate
-    du_ref[...] = d_up
+    units = hid_ref.shape[1]
+    route = jnp.zeros((rows, 1), f32)
+    for at in range(0, units, 256):
+        part = slice(at, at + 256)
+        gate = nn(tok_ref[...], gate_ref[:, part])
+        up = nn(tok_ref[...], up_ref[:, part])
+        back = nt(grad_ref[...], down_ref[part, :])
+        sig = jax.nn.sigmoid(gate)
+        silu = gate * sig
+        hidden = (silu * up).astype(bf16)
+        hid_ref[:, part] = hidden
+        route += jnp.sum(hidden.astype(f32) * back, axis=1, keepdims=True)
+        dg_ref[:, part] = (back * up * sig * (1.0 + gate * (1.0 - sig))).astype(bf16)
+        du_ref[:, part] = (back * silu).astype(bf16)
+    d_gate = dg_ref[...]
+    d_up = du_ref[...]
     for at in range(0, width, 512):
         cols = slice(at, at + 512)
         out_ref[:, cols] = (nt(d_gate, gate_ref[cols, :]) + nt(d_up, up_ref[cols, :])).astype(bf16)
@@ -157,7 +169,7 @@
     )(x, x, gate, up, down, counts)
 
 
-def tail_kernel(scale, pick_ref, back_ref, extra_ref, w_ref, sum_ref, tok_ref, prob_ref, acc, route_s, load_s):
+def tail_kernel(sizes, scale, pick_ref, back_ref, extra_ref, w_ref, sum_ref, tok_ref, prob_ref, acc, route_s, load_s):
     step = pl.program_id(0)
     rows = back_ref.shape[0]
     experts = w_ref.shape[1]
@@ -175,7 +187,8 @@
     first = iota((rows, LANES), 1) % (LANES // CAP) == 0
     high = jnp.sum(jnp.where(jnp.logical_and(first, turn == 4), extra, 0.0), axis=1, keepdims=True)
     low = jnp.sum(jnp.where(jnp.logical_and(first, turn == 5), extra, 0.0), axis=1, keepdims=True)
-    own = (iota((rows, experts), 0) + step * rows) // CAP == iota((rows, experts), 1)
+    slot = iota((rows, experts), 0) + step * rows
+    own = expert_of(slot, *sizes) == iota((rows, experts), 1)
     route_s[...] += nn(pick, jnp.where(own, high, 0.0).astype(bf16)) + nn(
         pick, jnp.where(own, low, 0.0).astype(bf16)
     )
@@ -193,14 +206,14 @@
         prob_ref[...] = jnp.where(named, (route - mean) / total, 0.0) + load_s[...] * scale
 
 
-def collect_rows(scale, pick, back, weight, total):
+def collect_rows(sizes, scale, pick, back, weight, total):
     toks, slots = pick.shape
     experts = weight.shape[1]
     width = back.shape[1] - LANES
     rows = 256
     whole = lambda shape: pl.BlockSpec(shape, lambda i: (0, 0))
     return pl.pallas_call(
-        lambda *refs: tail_kernel(scale, *refs),
+        functools.partial(tail_kernel, sizes, scale),
         grid=(slots // rows,),
         in_specs=[
             pl.BlockSpec((toks, rows), lambda i: (0, i)),
@@ -224,7 +237,7 @@
 def exchange(rows, devices):
     slots, width = rows.shape
     moved = lax.all_to_all(
-        rows.reshape(devices, slots // devices, width), AXES, split_axis=0, concat_axis=0, tiled=True
+        rows.reshape(devices, slots // devices, width), ORDER, split_axis=0, concat_axis=0, tiled=True
     )
     return moved.reshape(slots, width)
 
@@ -232,8 +245,9 @@
 def on_device(tokens, grad_out, probs, expert_ids, w_gate, w_up, w_down):
     toks, width = tokens.shape
     experts = probs.shape[1]
-    devices = lax.axis_size("dp") * lax.axis_size("expert")
-    x, pick, weight, total, counts = send_rows(expert_ids, probs, tokens, grad_out)
+    sizes = (lax.axis_size("dp"), lax.axis_size("expert"))
+    devices = sizes[0] * sizes[1]
+    x, pick, weight, total, counts = send_rows(sizes, expert_ids, probs, tokens, grad_out)
     x = exchange(x, devices)
     gate, up, down = [in_vmem(w[0]) for w in (w_gate, w_up, w_down)]
     out, hidden, d_gate_pre, d_up_pre = expert_rows(x, gate, up, down, counts)
@@ -242,7 +256,7 @@
     d_up = tn(x[:, :width], d_up_pre).astype(bf16)
     d_down = tn(hidden, x[:, width:]).astype(bf16)
     scale = aux_weight * experts / (devices * toks * expert_ids.shape[1])
-    d_tokens, d_probs = collect_rows(scale, pick, back, weight, total)
+    d_tokens, d_probs = collect_rows(sizes, scale, pick, back, weight, total)
     return (d_tokens, d_probs, d_gate[None], d_up[None], d_down[None])
 
 

time: 200 us -> 205 us (1.025)
  starting transfers between devices: 5.18 us -> 7.7 us
    all_to_all x1, starting transfers between devices: 5.18 us -> 7.7 us  [exchange(): lax.all_to_all(rows.reshape(devices, slots // devices, width), ORDER, spl...]
where the time goes in v2:
time: 205 us; the launch traced here: 204 us
  blocking collectives  110 us (54%)
  waiting for transfers between devices  35.4 us (17%)
  Pallas kernels  30.6 us (15%)
  matrix products  19.9 us (10%)
  starting transfers between devices  7.7 us (4%)
    all_to_all x1, blocking collectives, exchange(): lax.all_to_all(rows.reshape(devices, slots // devices, width), ORDER, spl...  110 us
    all_to_all x1, waiting for transfers between devices, exchange(): lax.all_to_all(rows.reshape(devices, slots // devices, width), ORDER, spl...  35.4 us
    pallas_call x1, Pallas kernels, expert_rows(): pl.pallas_call(expert_kernel, grid=(slots // rows,), in_specs=[block(widt...  20.1 us
    dot_general x3, matrix products, tn(): lax.dot_general(left, right, (((0,), (0,)), ((), ())), preferred_element_...  19.9 us
    all_to_all x1, starting transfers between devices, exchange(): lax.all_to_all(rows.reshape(devices, slots // devices, width), ORDER, spl...  7.7 us
    pallas_call x1, Pallas kernels, send_rows(): pl.pallas_call(functools.partial(send_kernel, sizes), grid=(slots // rows...  5.4 us
    pallas_call x1, Pallas kernels, collect_rows(): pl.pallas_call(functools.partial(tail_kernel, sizes, scale), grid=(slots...  5.09 us
  transfers between devices with their start and end apart: 1, of which 1 were waited for; matrix products, arithmetic and copies ran while one was open for 10% of the time, Pallas kernels for 0%

profile of v2, /device:TPU:1, one launch (start us, length us, event | category | flops | bytes accessed | tf_op | source)
XLA Modules:
  0.0 204.3 jit_solution(10707559702939049392)
XLA Ops:
  0.6 5.4 %send_rows.1 = (bf16[1024,4096]{1,0:T(8,128)(2,1)S(1)}, bf16[64,1024]{1,0:T(8,128)(2,1)S(1)}, f32[64,128]{1,0:T(8,128)S(1)}, f32[64,128]{1,0:T(8,128)S(1)}, f32[256,128]{1,0:T(8,128)S(1)}) custom-call(s32[8,64]{1,0:T(8,128)} %bitcast.29, f32[64,128]{1,0:T(8,128)} %probs_ref.1, bf16[64,2048]{1,0:T(8,128)(2,1)} %tok_ref.1, bf16[64,2048]{1,0:T(8,128)(2,1)} %grad_ref.1), custom_call_target="tpu_custom_call" | custom-call | tf_op jit(solution)/shard_map/send_rows/pallas_call | solution.py:96
  6.0 0.0 copy-start.3
  6.1 0.0 copy-start
  6.1 0.0 copy-start.1
  6.1 0.0 copy-start.2
  6.1 109.8 %all_to_all.10 = bf16[128,8,4096]{2,1,0:T(8,128)(2,1)} all-to-all(bf16[128,8,4096]{2,1,0:T(8,128)(2,1)S(1)} %bitcast.17), channel_id=1, replica_groups=mesh['dp'=8,'expert'=16] {'expert','dp'}, dimensions={0} | all-to-all | bytes 16777216 | tf_op jit(solution)/shard_map/all_to_all | solution.py:239
  115.9 0.0 copy-done.3
  115.9 0.0 copy-done
  115.9 0.0 copy-done.1
  115.9 0.0 copy-done.2
  115.9 20.1 %expert_rows.1 = (bf16[1024,2176]{1,0:T(8,128)(2,1)}, bf16[1024,768]{1,0:T(8,128)(2,1)}, bf16[1024,768]{1,0:T(8,128)(2,1)}, bf16[1024,768]{1,0:T(8,128)(2,1)}) custom-call(bf16[1024,4096]{1,0:T(8,128)(2,1)} %bitcast.21, bf16[1024,4096]{1,0:T(8,128)(2,1)} %bitcast.22, bf16[2048,768]{1,0:T(8,128)(2,1)S(1)} %bitcast.18, bf16[2048,768]{1,0:T(8,128)(2,1)S(1)} %bitcast.19, ...), custom_call_target="tpu_custom_call" | custom-call | tf_op jit(solution)/shard_map/expert_rows/pallas_call | solution.py:154
  136.1 0.0 copy-start.6
  136.1 7.7 %all-to-all-start.1 = ((bf16[128,8,2176]{2,1,0:T(8,128)(2,1)}), bf16[128,8,2176]{2,1,0:T(8,128)(2,1)}, u32[]{:S(2)}, u32[]{:S(2)}) async-start(bf16[128,8,2176]{2,1,0:T(8,128)(2,1)} %bitcast.28), calls=%async_computation.1 | async-start | bytes 8912896 | tf_op jit(solution)/shard_map/all_to_all | solution.py:239
  143.8 0.0 copy-done.6
  143.8 0.0 copy-start.5
  143.8 0.0 slice-start
  143.8 7.5 %fusion.21 = bf16[1,2048,768]{2,1,0:T(8,128)(2,1)} fusion(bf16[1024,768]{1,0:T(8,128)(2,1)S(1)} %copy-done.6, bf16[1024,4096]{1,0:T(8,128)(2,1)} %bitcast.23), kind=kOutput, calls=%fused_computation.11 | convolution fusion | flops 3222798336 | bytes 8912896 | tf_op jit(solution)/shard_map/dot_general | solution.py:32
  151.4 0.0 copy-done.5
  151.4 0.0 slice-start.1
  151.4 0.0 copy-start.4
  151.4 7.6 %fusion.18 = bf16[1,2048,768]{2,1,0:T(8,128)(2,1)} fusion(bf16[1024,768]{1,0:T(8,128)(2,1)S(1)} %copy-done.5, bf16[1024,4096]{1,0:T(8,128)(2,1)} %bitcast.24), kind=kOutput, calls=%fused_computation.10 | convolution fusion | flops 3222798336 | bytes 8912896 | tf_op jit(solution)/shard_map/dot_general | solution.py:32
  159.0 0.0 slice-done
  159.0 0.0 slice-done.1
  159.0 0.0 copy-done.4
  159.0 4.9 %fusion.15 = bf16[1,768,2048]{2,1,0:T(8,128)(2,1)} fusion(bf16[1024,768]{1,0:T(8,128)(2,1)S(1)} %copy-done.4, bf16[1024,4096]{1,0:T(8,128)(2,1)S(1)} %bitcast.27), kind=kOutput, calls=%fused_computation.9 | convolution fusion | flops 3222798336 | bytes 8912896 | tf_op jit(solution)/shard_map/dot_general | solution.py:32
  163.8 35.4 %all-to-all-done.1 = bf16[128,8,2176]{2,1,0:T(8,128)(2,1)} async-done(((bf16[128,8,2176]{2,1,0:T(8,128)(2,1)}), bf16[128,8,2176]{2,1,0:T(8,128)(2,1)}, u32[]{:S(2)}, u32[]{:S(2)}) %all-to-all-start.1) | async-done | bytes 4456480 | tf_op jit(solution)/shard_map/all_to_all | solution.py:239
  199.2 5.1 %collect_rows.1 = (bf16[64,2048]{1,0:T(8,128)(2,1)}, f32[64,128]{1,0:T(8,128)}) custom-call(bf16[64,1024]{1,0:T(8,128)(2,1)S(1)} %get-tuple-element.16.pick_ref, bf16[1024,2176]{1,0:T(8,128)(2,1)} %bitcast.7.back_ref.extra_ref, bf16[1024,2176]{1,0:T(8,128)(2,1)} %bitcast.7.back_ref.extra_ref, f32[64,128]{1,0:T(8,128)S(1)} %get-tuple-element.20.w_ref, ...), custom_call_target="tpu_custom_call" | custom-call | tf_op jit(solution)/shard_map/collect_rows/pallas_call | solution.py:215
  (1 shorter events, 0.0 us)
Async XLA Ops:
  6.0 109.9 %copy-start.3 = (f32[256,128]{1,0:T(8,128)}, f32[256,128]{1,0:T(8,128)S(1)}, u32[]{:S(2)}) copy-start(f32[256,128]{1,0:T(8,128)S(1)} %get-tuple-element.18.cnt_ref) | copy-start | bytes 393220
  6.1 109.9 %copy-start = (bf16[1,2048,768]{2,1,0:T(8,128)(2,1)S(1)}, bf16[1,2048,768]{2,1,0:T(8,128)(2,1)}, u32[]{:S(2)}) copy-start(bf16[1,2048,768]{2,1,0:T(8,128)(2,1)} %param.11) | copy-start | bytes 9437188
  6.1 109.9 %copy-start.1 = (bf16[1,2048,768]{2,1,0:T(8,128)(2,1)S(1)}, bf16[1,2048,768]{2,1,0:T(8,128)(2,1)}, u32[]{:S(2)}) copy-start(bf16[1,2048,768]{2,1,0:T(8,128)(2,1)} %param.12) | copy-start | bytes 9437188
  6.1 109.9 %copy-start.2 = (bf16[1,768,2048]{2,1,0:T(8,128)(2,1)S(1)}, bf16[1,768,2048]{2,1,0:T(8,128)(2,1)}, u32[]{:S(2)}) copy-start(bf16[1,768,2048]{2,1,0:T(8,128)(2,1)} %param.13) | copy-start | bytes 9437188
  136.1 7.7 %copy-start.6 = (bf16[1024,768]{1,0:T(8,128)(2,1)S(1)}, bf16[1024,768]{1,0:T(8,128)(2,1)}, u32[]{:S(2)}) copy-start(bf16[1024,768]{1,0:T(8,128)(2,1)} %get-tuple-element.24) | copy-start | bytes 4718596
  136.1 63.1 %all-to-all-start.1 = ((bf16[128,8,2176]{2,1,0:T(8,128)(2,1)}), bf16[128,8,2176]{2,1,0:T(8,128)(2,1)}, u32[]{:S(2)}, u32[]{:S(2)}) async-start(bf16[128,8,2176]{2,1,0:T(8,128)(2,1)} %bitcast.28), calls=%async_computation.1 | async-start | bytes 8912896 | tf_op jit(solution)/shard_map/all_to_all | solution.py:239
  143.8 7.6 %copy-start.5 = (bf16[1024,768]{1,0:T(8,128)(2,1)S(1)}, bf16[1024,768]{1,0:T(8,128)(2,1)}, u32[]{:S(2)}) copy-start(bf16[1024,768]{1,0:T(8,128)(2,1)} %get-tuple-element.25) | copy-start | bytes 4718596
  143.8 15.1 %slice-start = ((s8[8388608]{0:T(1024)(128)(4,1)}), s8[4194304]{0:T(1024)(128)(4,1)S(1)}, s32[]{:S(2)}) async-start(s8[8388608]{0:T(1024)(128)(4,1)} %bitcast.25), calls=%async_computation.2 | async-start | bytes 8388608
  151.4 7.6 %slice-start.1 = ((s8[8388608]{0:T(1024)(128)(4,1)}), s8[4194304]{0:T(1024)(128)(4,1)S(1)}, s32[]{:S(2)}) async-start(s8[8388608]{0:T(1024)(128)(4,1)} %bitcast.25), calls=%async_computation.3 | async-start | bytes 8388608
  151.4 7.6 %copy-start.4 = (bf16[1024,768]{1,0:T(8,128)(2,1)S(1)}, bf16[1024,768]{1,0:T(8,128)(2,1)}, u32[]{:S(2)}) copy-start(bf16[1024,768]{1,0:T(8,128)(2,1)} %get-tuple-element.26) | copy-start | bytes 4718596

commit v3 on v2

v3 whole, which is shorter than its diff:
```python
import functools

import jax
import jax.numpy as jnp
from jax import lax
from jax.experimental import pallas as pl
from jax.experimental.pallas import tpu as pltpu
from jax.sharding import PartitionSpec as P

aux_weight = 1.0
CAP = 8
LANES = 128
ROWS = 256
AXES = ("dp", "expert")
f32 = jnp.float32
bf16 = jnp.bfloat16


def iota(shape, dim):
    return lax.broadcasted_iota(jnp.int32, shape, dim)


def nn(left, right):
    return jnp.dot(left, right, preferred_element_type=f32)


def nt(left, right):
    return lax.dot_general(left, right, (((1,), (1,)), ((), ())), preferred_element_type=f32)


def tn(left, right):
    return lax.dot_general(left, right, (((0,), (0,)), ((), ())), preferred_element_type=f32)


def in_hbm(array):
    return pltpu.with_memory_space_constraint(array, pltpu.HBM)


def in_vmem(array):
    return pltpu.with_memory_space_constraint(array, pltpu.VMEM)


def send_kernel(
    ids_hbm, probs_hbm, tok_hbm, grad_hbm, x_ref, pick_ref, w_ref, sum_ref, cnt_ref, ids_ref, probs_ref, tok_ref, grad_ref, sems
):
    toks, experts = probs_ref.shape
    slots, width = x_ref.shape[0], tok_ref.shape[1]
    pairs = ((ids_hbm, ids_ref), (probs_hbm, probs_ref), (tok_hbm, tok_ref), (grad_hbm, grad_ref))
    copies = [pltpu.make_async_copy(a, b, sems.at[i]) for i, (a, b) in enumerate(pairs)]
    for copy in copies:
        copy.start()

    copies[0].wait()
    expert = iota((experts, toks), 0)
    member_t = ids_ref[0:1, :] == expert
    for k in range(1, ids_ref.shape[0]):
        member_t = jnp.logical_or(member_t, ids_ref[k : k + 1, :] == expert)
    same = (iota((experts, experts), 0) == iota((experts, experts), 1)).astype(bf16)
    named = tn(member_t.astype(f32).astype(bf16), same)
    member = named > 0.5
    before = (iota((toks, toks), 0) > iota((toks, toks), 1)).astype(bf16)
    rank = nn(before, named.astype(bf16))
    rank = jnp.where(member, rank, 100.0).astype(bf16)
    copies[1].wait()
    picked = jnp.where(member, probs_ref[...], 0.0)
    total = jnp.sum(picked, axis=1, keepdims=True)
    weight = (picked / total).astype(bf16)

    w_ref[...] = weight.astype(f32)
    sum_ref[...] = jnp.broadcast_to(total, sum_ref.shape)
    count = jnp.sum(named, axis=0, keepdims=True)
    mine = iota(cnt_ref.shape, 0) % CAP == iota(cnt_ref.shape, 1) // (LANES // CAP)
    cnt_ref[...] = jnp.where(mine, jnp.broadcast_to(count, cnt_ref.shape), 0.0)
    spread_t = (iota((experts, slots), 0) == iota((experts, slots), 1) // CAP).astype(bf16)
    pick_ref[...] = (nn(rank, spread_t) == (iota((toks, slots), 1) % CAP).astype(f32)).astype(bf16)

    spread = (iota((slots, experts), 0) // CAP == iota((slots, experts), 1)).astype(bf16)
    chosen = nt(spread, rank) == (iota((slots, toks), 0) % CAP).astype(f32)
    weights = nt(spread, weight)
    weights = jnp.where(chosen, weights, 0.0).astype(bf16)
    chosen = chosen.astype(bf16)
    copies[2].wait()
    copies[3].wait()
    for at in range(0, width, 512):
        x_ref[:, at : at + 512] = nn(chosen, tok_ref[:, at : at + 512]).astype(bf16)
        x_ref[:, width + at : width + at + 512] = nn(weights, grad_ref[:, at : at + 512]).astype(bf16)


def send_rows(ids, probs, tokens, grads):
    toks, width = tokens.shape
    experts = probs.shape[1]
    slots = experts * CAP
    arrays = [in_hbm(a) for a in (ids.T, probs, tokens, grads)]
    return pl.pallas_call(
        send_kernel,
        in_specs=[pl.BlockSpec(memory_space=pltpu.HBM)] * 4,
        out_specs=[pl.BlockSpec(memory_space=pltpu.VMEM)] * 5,
        out_shape=[
            jax.ShapeDtypeStruct((slots, 2 * width), bf16),
            jax.ShapeDtypeStruct((toks, slots), bf16),
            jax.ShapeDtypeStruct((toks, experts), f32),
            jax.ShapeDtypeStruct((toks, experts), f32),
            jax.ShapeDtypeStruct((ROWS, LANES), f32),
        ],
        scratch_shapes=[pltpu.VMEM(a.shape, a.dtype) for a in arrays] + [pltpu.SemaphoreType.DMA((4,))],
        compiler_params=pltpu.CompilerParams(vmem_limit_bytes=24 << 20),
        name="send_rows",
    )(*arrays)


def expert_kernel(tok_ref, grad_ref, gate_ref, up_ref, down_ref, cnt_ref, out_ref, hid_ref, dg_ref, du_ref):
    rows, width = tok_ref.shape
    units = hid_ref.shape[1]
    route = jnp.zeros((rows, 1), f32)
    for at in range(0, units, 256):
        part = slice(at, at + 256)
        gate = nn(tok_ref[...], gate_ref[:, part])
        up = nn(tok_ref[...], up_ref[:, part])
        back = nt(grad_ref[...], down_ref[part, :])
        sig = jax.nn.sigmoid(gate)
        silu = gate * sig
        hidden = (silu * up).astype(bf16)
        hid_ref[:, part] = hidden
        route += jnp.sum(hidden.astype(f32) * back, axis=1, keepdims=True)
        dg_ref[:, part] = (back * up * sig * (1.0 + gate * (1.0 - sig))).astype(bf16)
        du_ref[:, part] = (back * silu).astype(bf16)
    d_gate = dg_ref[...]
    d_up = du_ref[...]
    for at in range(0, width, 512):
        cols = slice(at, at + 512)
        out_ref[:, cols] = (nt(d_gate, gate_ref[cols, :]) + nt(d_up, up_ref[cols, :])).astype(bf16)
    high = route.astype(bf16).astype(f32)
    turn = (iota((rows, LANES), 1) // (LANES // CAP) - iota((rows, LANES), 0) % CAP + CAP) % CAP
    extra = jnp.where(turn == 4, high, jnp.where(turn == 5, route - high, cnt_ref[...]))
    out_ref[:, width:] = extra.astype(bf16)


def expert_rows(x, gate, up, down, counts):
    slots = x.shape[0]
    width, units = gate.shape
    rows = counts.shape[0]
    whole = lambda shape: pl.BlockSpec(shape, lambda i: (0, 0), pipeline_mode=pl.Buffered(1))
    block = lambda cols, at: pl.BlockSpec((rows, cols), lambda i: (i, at))
    part = jax.ShapeDtypeStruct((slots, units), bf16)
    return pl.pallas_call(
        expert_kernel,
        grid=(slots // rows,),
        in_specs=[
            block(width, 0),
            block(width, 1),
            whole(gate.shape),
            whole(up.shape),
            whole(down.shape),
            whole(counts.shape),
        ],
        out_specs=[block(width + LANES, 0), block(units, 0), block(units, 0), block(units, 0)],
        out_shape=[jax.ShapeDtypeStruct((slots, width + LANES), bf16), part, part, part],
        compiler_params=pltpu.CompilerParams(vmem_limit_bytes=50 << 20),
        name="expert_rows",
    )(x, x, gate, up, down, counts)


def tail_kernel(scale, pick_ref, w_ref, sum_ref, back_hbm, tok_ref, prob_ref, back_ref, acc, sems):
    slots, width = back_ref.shape[0], tok_ref.shape[1]
    experts = w_ref.shape[1]
    blocks = [pl.ds(at, ROWS) for at in range(0, slots, ROWS)]
    copies = [pltpu.make_async_copy(back_hbm.at[b], back_ref.at[b], sems.at[i]) for i, b in enumerate(blocks)]
    for copy in copies:
        copy.start()

    turn = (iota((ROWS, LANES), 1) // (LANES // CAP) - iota((ROWS, LANES), 0) % CAP + CAP) % CAP
    first = iota((ROWS, LANES), 1) % (LANES // CAP) == 0
    is_high = jnp.logical_and(first, turn == 4)
    is_low = jnp.logical_and(first, turn == 5)
    route = jnp.zeros(w_ref.shape, f32)
    load = jnp.zeros((1, LANES), f32)
    for i, block in enumerate(blocks):
        copies[i].wait()
        pick = pick_ref[:, i * ROWS : (i + 1) * ROWS]
        extra = back_ref[block, width:].astype(f32)
        high = jnp.sum(jnp.where(is_high, extra, 0.0), axis=1, keepdims=True)
        low = jnp.sum(jnp.where(is_low, extra, 0.0), axis=1, keepdims=True)
        own = (iota((ROWS, experts), 0) + i * ROWS) // CAP == iota((ROWS, experts), 1)
        route += nn(pick, jnp.where(own, high, 0.0).astype(bf16)) + nn(pick, jnp.where(own, low, 0.0).astype(bf16))
        load += jnp.sum(jnp.where(turn == 0, extra, 0.0), axis=0, keepdims=True)
        rows = nn(pick, back_ref[block, :width])
        if i == 0:
            acc[...] = rows
        elif i < len(blocks) - 1:
            acc[...] += rows
        else:
            tok_ref[...] = (acc[...] + rows).astype(bf16)
    weight = w_ref[...]
    member = weight > 0.0
    route = jnp.where(member, route / jnp.where(member, weight, 1.0), 0.0)
    route = route.astype(bf16).astype(f32)
    mean = jnp.sum(route * weight, axis=1, keepdims=True)
    prob_ref[...] = jnp.where(member, (route - mean) / sum_ref[...], 0.0) + load * scale


def collect_rows(scale, pick, back, weight, total):
    toks, slots = pick.shape
    experts = weight.shape[1]
    width = back.shape[1] - LANES
    return pl.pallas_call(
        functools.partial(tail_kernel, scale),
        in_specs=[pl.BlockSpec(memory_space=pltpu.VMEM)] * 3 + [pl.BlockSpec(memory_space=pltpu.HBM)],
        out_specs=[pl.BlockSpec(memory_space=pltpu.VMEM)] * 2,
        out_shape=[jax.ShapeDtypeStruct((toks, width), bf16), jax.ShapeDtypeStruct((toks, experts), f32)],
        scratch_shapes=[
            pltpu.VMEM(back.shape, bf16),
            pltpu.VMEM((toks, width), f32),
            pltpu.SemaphoreType.DMA((slots // ROWS,)),
        ],
        compiler_params=pltpu.CompilerParams(vmem_limit_bytes=24 << 20),
        name="collect_rows",
    )(pick, weight, total, in_hbm(back))


def exchange(rows, devices):
    slots, width = rows.shape
    moved = lax.all_to_all(
        rows.reshape(devices, slots // devices, width), AXES, split_axis=0, concat_axis=0, tiled=True
    )
    return moved.reshape(slots, width)


def on_device(tokens, grad_out, probs, expert_ids, w_gate, w_up, w_down):
    toks, width = tokens.shape
    experts = probs.shape[1]
    devices = lax.axis_size("dp") * lax.axis_size("expert")
    x, pick, weight, total, counts = send_rows(expert_ids, probs, tokens, grad_out)
    x = exchange(x, devices)
    gate, up, down = [in_vmem(w[0]) for w in (w_gate, w_up, w_down)]
    out, hidden, d_gate_pre, d_up_pre = expert_rows(x, gate, up, down, counts)
    back = exchange(out, devices)
    d_gate = tn(x[:, :width], d_gate_pre).astype(bf16)
    d_up = tn(x[:, :width], d_up_pre).astype(bf16)
    d_down = tn(hidden, x[:, width:]).astype(bf16)
    scale = aux_weight * experts / (devices * toks * expert_ids.shape[1])
    d_tokens, d_probs = collect_rows(scale, pick, back, weight, total)
    return (d_tokens, d_probs, d_gate[None], d_up[None], d_down[None])


def solution(mesh):
    flat = P(AXES, None)
    deep = P(AXES, None, None)
    return jax.shard_map(
        on_device,
        mesh=mesh,
        in_specs=(flat, flat, flat, flat, deep, deep, deep),
        out_specs=(flat, flat, deep, deep, deep),
        check_vma=False,
    )
```

time: 205 us -> 198 us (0.966)
  Pallas kernels: 30.6 us -> 27.4 us
  starting transfers between devices: 7.7 us -> 5.18 us
    pallas_call x2, Pallas kernels: 10.5 us -> 7.3 us  [the longest x1 3.8 us: send_rows(): pl.pallas_call(send_kernel, in_specs=[pl.BlockSpec(memory_space=pltpu.HBM...]
    all_to_all x1, starting transfers between devices: 7.7 us -> 5.18 us  [exchange(): lax.all_to_all(rows.reshape(devices, slots // devices, width), AXES, spli...]
where the time goes in v3:
time: 198 us; the launch traced here: 197 us
  blocking collectives  109 us (55%)
  waiting for transfers between devices  35.1 us (18%)
  Pallas kernels  27.4 us (14%)
  matrix products  20 us (10%)
  starting transfers between devices  5.18 us (3%)
    all_to_all x1, blocking collectives, exchange(): lax.all_to_all(rows.reshape(devices, slots // devices, width), AXES, spli...  109 us
    all_to_all x1, waiting for transfers between devices, exchange(): lax.all_to_all(rows.reshape(devices, slots // devices, width), AXES, spli...  35.1 us
    pallas_call x1, Pallas kernels, expert_rows(): pl.pallas_call(expert_kernel, grid=(slots // rows,), in_specs=[block(widt...  20.1 us
    dot_general x3, matrix products, tn(): lax.dot_general(left, right, (((0,), (0,)), ((), ())), preferred_element_...  20 us
    all_to_all x1, starting transfers between devices, exchange(): lax.all_to_all(rows.reshape(devices, slots // devices, width), AXES, spli...  5.18 us
  transfers between devices with their start and end apart: 1, of which 1 were waited for; matrix products, arithmetic and copies ran while one was open for 10% of the time, Pallas kernels for 0%

profile of v3, /device:TPU:1, one launch (start us, length us, event | category | flops | bytes accessed | tf_op | source)
XLA Modules:
  0.0 197.4 jit_solution(7944557660370066887)
XLA Ops:
  0.6 3.8 %send_rows.1 = (bf16[1024,4096]{1,0:T(8,128)(2,1)S(1)}, bf16[64,1024]{1,0:T(8,128)(2,1)S(1)}, f32[64,128]{1,0:T(8,128)S(1)}, f32[64,128]{1,0:T(8,128)S(1)}, f32[256,128]{1,0:T(8,128)S(1)}) custom-call(s32[8,64]{1,0:T(8,128)} %bitcast.29, f32[64,128]{1,0:T(8,128)} %probs_hbm.1, bf16[64,2048]{1,0:T(8,128)(2,1)} %tok_hbm.1, bf16[64,2048]{1,0:T(8,128)(2,1)} %grad_hbm.1), custom_call_target="tpu_custom_call" | custom-call | tf_op jit(solution)/shard_map/send_rows/pallas_call | solution.py:94
  4.4 0.0 copy-start.3
  4.4 0.0 copy-start
  4.5 0.0 copy-start.1
  4.5 0.0 copy-start.2
  4.5 108.8 %all_to_all.10 = bf16[128,8,4096]{2,1,0:T(8,128)(2,1)} all-to-all(bf16[128,8,4096]{2,1,0:T(8,128)(2,1)S(1)} %bitcast.17), channel_id=1, replica_groups=mesh['dp'=8,'expert'=16] {'dp','expert'}, dimensions={0} | all-to-all | bytes 16777216 | tf_op jit(solution)/shard_map/all_to_all | solution.py:222
  113.3 0.0 copy-done.3
  113.3 0.0 copy-done
  113.3 0.0 copy-done.1
  113.3 0.0 copy-done.2
  113.3 20.1 %expert_rows.1 = (bf16[1024,2176]{1,0:T(8,128)(2,1)}, bf16[1024,768]{1,0:T(8,128)(2,1)}, bf16[1024,768]{1,0:T(8,128)(2,1)}, bf16[1024,768]{1,0:T(8,128)(2,1)}) custom-call(bf16[1024,4096]{1,0:T(8,128)(2,1)} %bitcast.21, bf16[1024,4096]{1,0:T(8,128)(2,1)} %bitcast.22, bf16[2048,768]{1,0:T(8,128)(2,1)S(1)} %bitcast.18, bf16[2048,768]{1,0:T(8,128)(2,1)S(1)} %bitcast.19, ...), custom_call_target="tpu_custom_call" | custom-call | tf_op jit(solution)/shard_map/expert_rows/pallas_call | solution.py:145
  133.4 0.0 copy-start.6
  133.5 5.2 %all-to-all-start.1 = ((bf16[128,8,2176]{2,1,0:T(8,128)(2,1)}), bf16[128,8,2176]{2,1,0:T(8,128)(2,1)}, u32[]{:S(2)}, u32[]{:S(2)}) async-start(bf16[128,8,2176]{2,1,0:T(8,128)(2,1)} %bitcast.28), calls=%async_computation.1 | async-start | bytes 8912896 | tf_op jit(solution)/shard_map/all_to_all | solution.py:222
  138.6 0.0 copy-done.6
  138.7 0.0 copy-start.5
  138.7 0.0 slice-start
  138.7 7.5 %fusion.21 = bf16[1,2048,768]{2,1,0:T(8,128)(2,1)} fusion(bf16[1024,768]{1,0:T(8,128)(2,1)S(1)} %copy-done.6, bf16[1024,4096]{1,0:T(8,128)(2,1)} %bitcast.23), kind=kOutput, calls=%fused_computation.11 | convolution fusion | flops 3222798336 | bytes 8912896 | tf_op jit(solution)/shard_map/dot_general | solution.py:32
  146.2 0.0 copy-done.5
  146.2 0.0 slice-start.1
  146.2 0.0 copy-start.4
  146.2 7.6 %fusion.18 = bf16[1,2048,768]{2,1,0:T(8,128)(2,1)} fusion(bf16[1024,768]{1,0:T(8,128)(2,1)S(1)} %copy-done.5, bf16[1024,4096]{1,0:T(8,128)(2,1)} %bitcast.24), kind=kOutput, calls=%fused_computation.10 | convolution fusion | flops 3222798336 | bytes 8912896 | tf_op jit(solution)/shard_map/dot_general | solution.py:32
  153.8 0.0 slice-done
  153.8 0.0 slice-done.1
  153.8 0.0 copy-done.4
  153.8 4.9 %fusion.15 = bf16[1,768,2048]{2,1,0:T(8,128)(2,1)} fusion(bf16[1024,768]{1,0:T(8,128)(2,1)S(1)} %copy-done.4, bf16[1024,4096]{1,0:T(8,128)(2,1)S(1)} %bitcast.27), kind=kOutput, calls=%fused_computation.9 | convolution fusion | flops 3222798336 | bytes 8912896 | tf_op jit(solution)/shard_map/dot_general | solution.py:32
  158.7 35.1 %all-to-all-done.1 = bf16[128,8,2176]{2,1,0:T(8,128)(2,1)} async-done(((bf16[128,8,2176]{2,1,0:T(8,128)(2,1)}), bf16[128,8,2176]{2,1,0:T(8,128)(2,1)}, u32[]{:S(2)}, u32[]{:S(2)}) %all-to-all-start.1) | async-done | bytes 4456480 | tf_op jit(solution)/shard_map/all_to_all | solution.py:222
  193.8 3.5 %collect_rows.1 = (bf16[64,2048]{1,0:T(8,128)(2,1)}, f32[64,128]{1,0:T(8,128)}) custom-call(bf16[64,1024]{1,0:T(8,128)(2,1)S(1)} %get-tuple-element.16.pick_ref, f32[64,128]{1,0:T(8,128)S(1)} %get-tuple-element.17.w_ref, f32[64,128]{1,0:T(8,128)S(1)} %get-tuple-element.18.sum_ref, bf16[1024,2176]{1,0:T(8,128)(2,1)} %bitcast.7.back_hbm), custom_call_target="tpu_custom_call" | custom-call | tf_op jit(solution)/shard_map/collect_rows/pallas_call | solution.py:205
  (1 shorter events, 0.0 us)
Async XLA Ops:
  4.4 108.9 %copy-start.3 = (f32[256,128]{1,0:T(8,128)}, f32[256,128]{1,0:T(8,128)S(1)}, u32[]{:S(2)}) copy-start(f32[256,128]{1,0:T(8,128)S(1)} %get-tuple-element.20.cnt_ref) | copy-start | bytes 393220
  4.4 108.8 %copy-start = (bf16[1,2048,768]{2,1,0:T(8,128)(2,1)S(1)}, bf16[1,2048,768]{2,1,0:T(8,128)(2,1)}, u32[]{:S(2)}) copy-start(bf16[1,2048,768]{2,1,0:T(8,128)(2,1)} %param.11) | copy-start | bytes 9437188
  4.5 108.8 %copy-start.1 = (bf16[1,2048,768]{2,1,0:T(8,128)(2,1)S(1)}, bf16[1,2048,768]{2,1,0:T(8,128)(2,1)}, u32[]{:S(2)}) copy-start(bf16[1,2048,768]{2,1,0:T(8,128)(2,1)} %param.12) | copy-start | bytes 9437188
  4.5 108.8 %copy-start.2 = (bf16[1,768,2048]{2,1,0:T(8,128)(2,1)S(1)}, bf16[1,768,2048]{2,1,0:T(8,128)(2,1)}, u32[]{:S(2)}) copy-start(bf16[1,768,2048]{2,1,0:T(8,128)(2,1)} %param.13) | copy-start | bytes 9437188
  133.4 5.2 %copy-start.6 = (bf16[1024,768]{1,0:T(8,128)(2,1)S(1)}, bf16[1024,768]{1,0:T(8,128)(2,1)}, u32[]{:S(2)}) copy-start(bf16[1024,768]{1,0:T(8,128)(2,1)} %get-tuple-element.24) | copy-start | bytes 4718596
  133.5 60.3 %all-to-all-start.1 = ((bf16[128,8,2176]{2,1,0:T(8,128)(2,1)}), bf16[128,8,2176]{2,1,0:T(8,128)(2,1)}, u32[]{:S(2)}, u32[]{:S(2)}) async-start(bf16[128,8,2176]{2,1,0:T(8,128)(2,1)} %bitcast.28), calls=%async_computation.1 | async-start | bytes 8912896 | tf_op jit(solution)/shard_map/all_to_all | solution.py:222
  138.7 7.6 %copy-start.5 = (bf16[1024,768]{1,0:T(8,128)(2,1)S(1)}, bf16[1024,768]{1,0:T(8,128)(2,1)}, u32[]{:S(2)}) copy-start(bf16[1024,768]{1,0:T(8,128)(2,1)} %get-tuple-element.25) | copy-start | bytes 4718596
  138.7 15.1 %slice-start = ((s8[8388608]{0:T(1024)(128)(4,1)}), s8[4194304]{0:T(1024)(128)(4,1)S(1)}, s32[]{:S(2)}) async-start(s8[8388608]{0:T(1024)(128)(4,1)} %bitcast.25), calls=%async_computation.2 | async-start | bytes 8388608
  146.2 7.6 %slice-start.1 = ((s8[8388608]{0:T(1024)(128)(4,1)}), s8[4194304]{0:T(1024)(128)(4,1)S(1)}, s32[]{:S(2)}) async-start(s8[8388608]{0:T(1024)(128)(4,1)} %bitcast.25), calls=%async_computation.3 | async-start | bytes 8388608
  146.2 7.6 %copy-start.4 = (bf16[1024,768]{1,0:T(8,128)(2,1)S(1)}, bf16[1024,768]{1,0:T(8,128)(2,1)}, u32[]{:S(2)}) copy-start(bf16[1024,768]{1,0:T(8,128)(2,1)} %get-tuple-element.26) | copy-start | bytes 4718596

commit v4 on v3

--- a/solution.py
+++ b/solution.py
@@ -111,7 +111,7 @@
 def expert_kernel(tok_ref, grad_ref, gate_ref, up_ref, down_ref, cnt_ref, out_ref, hid_ref, dg_ref, du_ref):
     rows, width = tok_ref.shape
     units = hid_ref.shape[1]
-    route = jnp.zeros((rows, 1), f32)
+    terms = jnp.zeros((rows, LANES), f32)
     for at in range(0, units, 256):
         part = slice(at, at + 256)
         gate = nn(tok_ref[...], gate_ref[:, part])
@@ -121,7 +121,8 @@
         silu = gate * sig
         hidden = (silu * up).astype(bf16)
         hid_ref[:, part] = hidden
-        route += jnp.sum(hidden.astype(f32) * back, axis=1, keepdims=True)
+        term = hidden.astype(f32) * back
+        terms += term[:, :LANES] + term[:, LANES:]
         dg_ref[:, part] = (back * up * sig * (1.0 + gate * (1.0 - sig))).astype(bf16)
         du_ref[:, part] = (back * silu).astype(bf16)
     d_gate = dg_ref[...]
@@ -129,6 +130,7 @@
     for at in range(0, width, 512):
         cols = slice(at, at + 512)
         out_ref[:, cols] = (nt(d_gate, gate_ref[cols, :]) + nt(d_up, up_ref[cols, :])).astype(bf16)
+    route = jnp.sum(terms, axis=1, keepdims=True)
     high = route.astype(bf16).astype(f32)
     turn = (iota((rows, LANES), 1) // (LANES // CAP) - iota((rows, LANES), 0) % CAP + CAP) % CAP
     extra = jnp.where(turn == 4, high, jnp.where(turn == 5, route - high, cnt_ref[...]))
@@ -155,7 +157,7 @@
         ],
         out_specs=[block(width + LANES, 0), block(units, 0), block(units, 0), block(units, 0)],
         out_shape=[jax.ShapeDtypeStruct((slots, width + LANES), bf16), part, part, part],
-        compiler_params=pltpu.CompilerParams(vmem_limit_bytes=50 << 20),
+        compiler_params=pltpu.CompilerParams(vmem_limit_bytes=41 << 20),
         name="expert_rows",
     )(x, x, gate, up, down, counts)
 

time: 198 us -> 197 us (level)
  no operation moved by 1% of the time
where the time goes in v4:
time: 197 us
  blocking collectives  109 us (55%)
  waiting for transfers between devices  35.2 us (18%)
  Pallas kernels  27.2 us (14%)
  matrix products  19.9 us (10%)
  starting transfers between devices  5.04 us (3%)
    all_to_all x1, blocking collectives, exchange(): lax.all_to_all(rows.reshape(devices, slots // devices, width), AXES, spli...  109 us
    all_to_all x1, waiting for transfers between devices, exchange(): lax.all_to_all(rows.reshape(devices, slots // devices, width), AXES, spli...  35.2 us
    dot_general x3, matrix products, tn(): lax.dot_general(left, right, (((0,), (0,)), ((), ())), preferred_element_...  19.9 us
    pallas_call x1, Pallas kernels, expert_rows(): pl.pallas_call(expert_kernel, grid=(slots // rows,), in_specs=[block(widt...  19.9 us
    all_to_all x1, starting transfers between devices, exchange(): lax.all_to_all(rows.reshape(devices, slots // devices, width), AXES, spli...  5.04 us
  transfers between devices with their start and end apart: 1, of which 1 were waited for; matrix products, arithmetic and copies ran while one was open for 10% of the time, Pallas kernels for 0%

profile of v4, /device:TPU:1, one launch (start us, length us, event | category | flops | bytes accessed | tf_op | source)
XLA Modules:
  0.0 197.0 jit_solution(15659868016872184278)
XLA Ops:
  0.6 3.8 %send_rows.1 = (bf16[1024,4096]{1,0:T(8,128)(2,1)S(1)}, bf16[64,1024]{1,0:T(8,128)(2,1)S(1)}, f32[64,128]{1,0:T(8,128)S(1)}, f32[64,128]{1,0:T(8,128)S(1)}, f32[256,128]{1,0:T(8,128)S(1)}) custom-call(s32[8,64]{1,0:T(8,128)} %bitcast.29, f32[64,128]{1,0:T(8,128)} %probs_hbm.1, bf16[64,2048]{1,0:T(8,128)(2,1)} %tok_hbm.1, bf16[64,2048]{1,0:T(8,128)(2,1)} %grad_hbm.1), custom_call_target="tpu_custom_call" | custom-call | tf_op jit(solution)/shard_map/send_rows/pallas_call | solution.py:94
  4.4 0.0 copy-start
  4.4 0.0 copy-start.1
  4.5 0.0 copy-start.2
  4.5 108.8 %all_to_all.10 = bf16[128,8,4096]{2,1,0:T(8,128)(2,1)} all-to-all(bf16[128,8,4096]{2,1,0:T(8,128)(2,1)S(1)} %bitcast.17), channel_id=1, replica_groups=mesh['dp'=8,'expert'=16] {'dp','expert'}, dimensions={0} | all-to-all | bytes 16777216 | tf_op jit(solution)/shard_map/all_to_all | solution.py:224
  113.3 0.0 copy-done
  113.3 0.0 copy-done.1
  113.3 0.0 copy-done.2
  113.3 19.9 %expert_rows.1 = (bf16[1024,2176]{1,0:T(8,128)(2,1)}, bf16[1024,768]{1,0:T(8,128)(2,1)S(1)}, bf16[1024,768]{1,0:T(8,128)(2,1)S(1)}, bf16[1024,768]{1,0:T(8,128)(2,1)}) custom-call(bf16[1024,4096]{1,0:T(8,128)(2,1)} %bitcast.21, bf16[1024,4096]{1,0:T(8,128)(2,1)} %bitcast.22, bf16[2048,768]{1,0:T(8,128)(2,1)S(1)} %bitcast.18, bf16[2048,768]{1,0:T(8,128)(2,1)S(1)} %bitcast.19, ...), custom_call_target="tpu_custom_call" | custom-call | tf_op jit(solution)/shard_map/expert_rows/pallas_call | solution.py:147
  133.1 5.0 %all-to-all-start.1 = ((bf16[128,8,2176]{2,1,0:T(8,128)(2,1)}), bf16[128,8,2176]{2,1,0:T(8,128)(2,1)}, u32[]{:S(2)}, u32[]{:S(2)}) async-start(bf16[128,8,2176]{2,1,0:T(8,128)(2,1)} %bitcast.28), calls=%async_computation.1 | async-start | bytes 8912896 | tf_op jit(solution)/shard_map/all_to_all | solution.py:224
  138.2 0.0 copy-start.3
  138.2 0.0 slice-start
  138.2 7.5 %fusion.21 = bf16[1,2048,768]{2,1,0:T(8,128)(2,1)} fusion(bf16[1024,768]{1,0:T(8,128)(2,1)S(1)} %get-tuple-element.24, bf16[1024,4096]{1,0:T(8,128)(2,1)} %bitcast.23), kind=kOutput, calls=%fused_computation.11 | convolution fusion | flops 3222798336 | bytes 8912896 | tf_op jit(solution)/shard_map/dot_general | solution.py:32
  145.7 0.0 copy-done.3
  145.8 0.0 slice-start.1
  145.8 7.6 %fusion.18 = bf16[1,2048,768]{2,1,0:T(8,128)(2,1)} fusion(bf16[1024,768]{1,0:T(8,128)(2,1)S(1)} %copy-done.3, bf16[1024,4096]{1,0:T(8,128)(2,1)} %bitcast.24), kind=kOutput, calls=%fused_computation.10 | convolution fusion | flops 3222798336 | bytes 8912896 | tf_op jit(solution)/shard_map/dot_general | solution.py:32
  153.3 0.0 slice-done
  153.3 0.0 slice-done.1
  153.3 4.8 %fusion.15 = bf16[1,768,2048]{2,1,0:T(8,128)(2,1)} fusion(bf16[1024,768]{1,0:T(8,128)(2,1)S(1)} %get-tuple-element.26, bf16[1024,4096]{1,0:T(8,128)(2,1)S(1)} %bitcast.27), kind=kOutput, calls=%fused_computation.9 | convolution fusion | flops 3222798336 | bytes 8912896 | tf_op jit(solution)/shard_map/dot_general | solution.py:32
  158.1 35.2 %all-to-all-done.1 = bf16[128,8,2176]{2,1,0:T(8,128)(2,1)} async-done(((bf16[128,8,2176]{2,1,0:T(8,128)(2,1)}), bf16[128,8,2176]{2,1,0:T(8,128)(2,1)}, u32[]{:S(2)}, u32[]{:S(2)}) %all-to-all-start.1) | async-done | bytes 4456480 | tf_op jit(solution)/shard_map/all_to_all | solution.py:224
  193.3 3.5 %collect_rows.1 = (bf16[64,2048]{1,0:T(8,128)(2,1)}, f32[64,128]{1,0:T(8,128)}) custom-call(bf16[64,1024]{1,0:T(8,128)(2,1)S(1)} %get-tuple-element.16.pick_ref, f32[64,128]{1,0:T(8,128)S(1)} %get-tuple-element.17.w_ref, f32[64,128]{1,0:T(8,128)S(1)} %get-tuple-element.18.sum_ref, bf16[1024,2176]{1,0:T(8,128)(2,1)} %bitcast.7.back_hbm), custom_call_target="tpu_custom_call" | custom-call | tf_op jit(solution)/shard_map/collect_rows/pallas_call | solution.py:207
  (1 shorter events, 0.0 us)
Async XLA Ops:
  4.4 108.8 %copy-start = (bf16[1,2048,768]{2,1,0:T(8,128)(2,1)S(1)}, bf16[1,2048,768]{2,1,0:T(8,128)(2,1)}, u32[]{:S(2)}) copy-start(bf16[1,2048,768]{2,1,0:T(8,128)(2,1)} %param.11) | copy-start | bytes 9437188
  4.4 108.8 %copy-start.1 = (bf16[1,2048,768]{2,1,0:T(8,128)(2,1)S(1)}, bf16[1,2048,768]{2,1,0:T(8,128)(2,1)}, u32[]{:S(2)}) copy-start(bf16[1,2048,768]{2,1,0:T(8,128)(2,1)} %param.12) | copy-start | bytes 9437188
  4.5 108.8 %copy-start.2 = (bf16[1,768,2048]{2,1,0:T(8,128)(2,1)S(1)}, bf16[1,768,2048]{2,1,0:T(8,128)(2,1)}, u32[]{:S(2)}) copy-start(bf16[1,768,2048]{2,1,0:T(8,128)(2,1)} %param.13) | copy-start | bytes 9437188
  133.1 60.2 %all-to-all-start.1 = ((bf16[128,8,2176]{2,1,0:T(8,128)(2,1)}), bf16[128,8,2176]{2,1,0:T(8,128)(2,1)}, u32[]{:S(2)}, u32[]{:S(2)}) async-start(bf16[128,8,2176]{2,1,0:T(8,128)(2,1)} %bitcast.28), calls=%async_computation.1 | async-start | bytes 8912896 | tf_op jit(solution)/shard_map/all_to_all | solution.py:224
  138.2 7.6 %copy-start.3 = (bf16[1024,768]{1,0:T(8,128)(2,1)S(1)}, bf16[1024,768]{1,0:T(8,128)(2,1)}, u32[]{:S(2)}) copy-start(bf16[1024,768]{1,0:T(8,128)(2,1)} %get-tuple-element.25) | copy-start | bytes 4718596
  138.2 15.1 %slice-start = ((s8[8388608]{0:T(1024)(128)(4,1)}), s8[4194304]{0:T(1024)(128)(4,1)S(1)}, s32[]{:S(2)}) async-start(s8[8388608]{0:T(1024)(128)(4,1)} %bitcast.25), calls=%async_computation.2 | async-start | bytes 8388608
  145.8 7.6 %slice-start.1 = ((s8[8388608]{0:T(1024)(128)(4,1)}), s8[4194304]{0:T(1024)(128)(4,1)S(1)}, s32[]{:S(2)}) async-start(s8[8388608]{0:T(1024)(128)(4,1)} %bitcast.25), calls=%async_computation.3 | async-start | bytes 8388608

commit v5 on v4

--- a/solution.py
+++ b/solution.py
@@ -162,42 +162,47 @@
     )(x, x, gate, up, down, counts)
 
 
-def tail_kernel(scale, pick_ref, w_ref, sum_ref, back_hbm, tok_ref, prob_ref, back_ref, acc, sems):
-    slots, width = back_ref.shape[0], tok_ref.shape[1]
+def tail_kernel(scale, pick_ref, w_ref, sum_ref, back_hbm, tok_ref, prob_ref, extra_ref, back_ref, acc, sems):
+    slots, width = back_ref.shape
     experts = w_ref.shape[1]
     blocks = [pl.ds(at, ROWS) for at in range(0, slots, ROWS)]
-    copies = [pltpu.make_async_copy(back_hbm.at[b], back_ref.at[b], sems.at[i]) for i, b in enumerate(blocks)]
+    first = pltpu.make_async_copy(back_hbm.at[:, pl.ds(width, LANES)], extra_ref, sems.at[len(blocks)])
+    copies = [
+        pltpu.make_async_copy(back_hbm.at[b, pl.ds(0, width)], back_ref.at[b], sems.at[i]) for i, b in enumerate(blocks)
+    ]
+    first.start()
     for copy in copies:
         copy.start()
 
-    turn = (iota((ROWS, LANES), 1) // (LANES // CAP) - iota((ROWS, LANES), 0) % CAP + CAP) % CAP
-    first = iota((ROWS, LANES), 1) % (LANES // CAP) == 0
-    is_high = jnp.logical_and(first, turn == 4)
-    is_low = jnp.logical_and(first, turn == 5)
-    route = jnp.zeros(w_ref.shape, f32)
-    load = jnp.zeros((1, LANES), f32)
+    first.wait()
+    row = iota((slots, LANES), 0)
+    lane = iota((slots, LANES), 1)
+    turn = (lane // (LANES // CAP) - row % CAP + CAP) % CAP
+    extra = extra_ref[...].astype(f32)
+    head = jnp.where(lane % (LANES // CAP) == 0, extra, 0.0)
+    own = row // CAP == lane
+    ones = jnp.ones((LANES, experts), bf16)
+    high = nn(jnp.where(turn == 4, head, 0.0).astype(bf16), ones)
+    low = nn(jnp.where(turn == 5, head, 0.0).astype(bf16), ones)
+    route = nn(pick_ref[...], jnp.where(own, high, 0.0).astype(bf16))
+    route += nn(pick_ref[...], jnp.where(own, low, 0.0).astype(bf16))
+    load = jnp.sum(jnp.where(turn == 0, extra, 0.0), axis=0, keepdims=True)
+    weight = w_ref[...]
+    member = weight > 0.0
+    route = jnp.where(member, route / jnp.where(member, weight, 1.0), 0.0)
+    route = route.astype(bf16).astype(f32)
+    mean = jnp.sum(route * weight, axis=1, keepdims=True)
+    prob_ref[...] = jnp.where(member, (route - mean) / sum_ref[...], 0.0) + load * scale
+
     for i, block in enumerate(blocks):
         copies[i].wait()
-        pick = pick_ref[:, i * ROWS : (i + 1) * ROWS]
-        extra = back_ref[block, width:].astype(f32)
-        high = jnp.sum(jnp.where(is_high, extra, 0.0), axis=1, keepdims=True)
-        low = jnp.sum(jnp.where(is_low, extra, 0.0), axis=1, keepdims=True)
-        own = (iota((ROWS, experts), 0) + i * ROWS) // CAP == iota((ROWS, experts), 1)
-        route += nn(pick, jnp.where(own, high, 0.0).astype(bf16)) + nn(pick, jnp.where(own, low, 0.0).astype(bf16))
-        load += jnp.sum(jnp.where(turn == 0, extra, 0.0), axis=0, keepdims=True)
-        rows = nn(pick, back_ref[block, :width])
+        rows = nn(pick_ref[:, i * ROWS : (i + 1) * ROWS], back_ref[block, :])
         if i == 0:
             acc[...] = rows
         elif i < len(blocks) - 1:
             acc[...] += rows
         else:
             tok_ref[...] = (acc[...] + rows).astype(bf16)
-    weight = w_ref[...]
-    member = weight > 0.0
-    route = jnp.where(member, route / jnp.where(member, weight, 1.0), 0.0)
-    route = route.astype(bf16).astype(f32)
-    mean = jnp.sum(route * weight, axis=1, keepdims=True)
-    prob_ref[...] = jnp.where(member, (route - mean) / sum_ref[...], 0.0) + load * scale
 
 
 def collect_rows(scale, pick, back, weight, total):
@@ -210,9 +215,10 @@
         out_specs=[pl.BlockSpec(memory_space=pltpu.VMEM)] * 2,
         out_shape=[jax.ShapeDtypeStruct((toks, width), bf16), jax.ShapeDtypeStruct((toks, experts), f32)],
         scratch_shapes=[
-            pltpu.VMEM(back.shape, bf16),
+            pltpu.VMEM((slots, LANES), bf16),
+            pltpu.VMEM((slots, width), bf16),
             pltpu.VMEM((toks, width), f32),
-            pltpu.SemaphoreType.DMA((slots // ROWS,)),
+            pltpu.SemaphoreType.DMA((slots // ROWS + 1,)),
         ],
         compiler_params=pltpu.CompilerParams(vmem_limit_bytes=24 << 20),
         name="collect_rows",

time: 197 us -> 197 us (level)
  no operation moved by 1% of the time
where the time goes in v5:
time: 197 us
  blocking collectives  109 us (55%)
  waiting for transfers between devices  35.2 us (18%)
  Pallas kernels  27 us (14%)
  matrix products  19.9 us (10%)
  starting transfers between devices  5.04 us (3%)
    all_to_all x1, blocking collectives, exchange(): lax.all_to_all(rows.reshape(devices, slots // devices, width), AXES, spli...  109 us
    all_to_all x1, waiting for transfers between devices, exchange(): lax.all_to_all(rows.reshape(devices, slots // devices, width), AXES, spli...  35.2 us
    dot_general x3, matrix products, tn(): lax.dot_general(left, right, (((0,), (0,)), ((), ())), preferred_element_...  19.9 us
    pallas_call x1, Pallas kernels, expert_rows(): pl.pallas_call(expert_kernel, grid=(slots // rows,), in_specs=[block(widt...  19.9 us
    all_to_all x1, starting transfers between devices, exchange(): lax.all_to_all(rows.reshape(devices, slots // devices, width), AXES, spli...  5.04 us
  transfers between devices with their start and end apart: 1, of which 1 were waited for; matrix products, arithmetic and copies ran while one was open for 10% of the time, Pallas kernels for 0%

profile of v5, /device:TPU:1, one launch (start us, length us, event | category | flops | bytes accessed | tf_op | source)
XLA Modules:
  0.0 196.8 jit_solution(4630912704477186639)
XLA Ops:
  0.6 3.8 %send_rows.1 = (bf16[1024,4096]{1,0:T(8,128)(2,1)S(1)}, bf16[64,1024]{1,0:T(8,128)(2,1)S(1)}, f32[64,128]{1,0:T(8,128)S(1)}, f32[64,128]{1,0:T(8,128)S(1)}, f32[256,128]{1,0:T(8,128)S(1)}) custom-call(s32[8,64]{1,0:T(8,128)} %bitcast.29, f32[64,128]{1,0:T(8,128)} %probs_hbm.1, bf16[64,2048]{1,0:T(8,128)(2,1)} %tok_hbm.1, bf16[64,2048]{1,0:T(8,128)(2,1)} %grad_hbm.1), custom_call_target="tpu_custom_call" | custom-call | tf_op jit(solution)/shard_map/send_rows/pallas_call | solution.py:94
  4.4 0.0 copy-start
  4.4 0.0 copy-start.1
  4.5 0.0 copy-start.2
  4.5 108.8 %all_to_all.10 = bf16[128,8,4096]{2,1,0:T(8,128)(2,1)} all-to-all(bf16[128,8,4096]{2,1,0:T(8,128)(2,1)S(1)} %bitcast.17), channel_id=1, replica_groups=mesh['dp'=8,'expert'=16] {'dp','expert'}, dimensions={0} | all-to-all | bytes 16777216 | tf_op jit(solution)/shard_map/all_to_all | solution.py:230
  113.3 0.0 copy-done
  113.3 0.0 copy-done.1
  113.3 0.0 copy-done.2
  113.3 19.9 %expert_rows.1 = (bf16[1024,2176]{1,0:T(8,128)(2,1)}, bf16[1024,768]{1,0:T(8,128)(2,1)S(1)}, bf16[1024,768]{1,0:T(8,128)(2,1)S(1)}, bf16[1024,768]{1,0:T(8,128)(2,1)}) custom-call(bf16[1024,4096]{1,0:T(8,128)(2,1)} %bitcast.21, bf16[1024,4096]{1,0:T(8,128)(2,1)} %bitcast.22, bf16[2048,768]{1,0:T(8,128)(2,1)S(1)} %bitcast.18, bf16[2048,768]{1,0:T(8,128)(2,1)S(1)} %bitcast.19, ...), custom_call_target="tpu_custom_call" | custom-call | tf_op jit(solution)/shard_map/expert_rows/pallas_call | solution.py:147
  133.1 5.0 %all-to-all-start.1 = ((bf16[128,8,2176]{2,1,0:T(8,128)(2,1)}), bf16[128,8,2176]{2,1,0:T(8,128)(2,1)}, u32[]{:S(2)}, u32[]{:S(2)}) async-start(bf16[128,8,2176]{2,1,0:T(8,128)(2,1)} %bitcast.28), calls=%async_computation.1 | async-start | bytes 8912896 | tf_op jit(solution)/shard_map/all_to_all | solution.py:230
  138.2 0.0 copy-start.3
  138.2 0.0 slice-start
  138.2 7.5 %fusion.21 = bf16[1,2048,768]{2,1,0:T(8,128)(2,1)} fusion(bf16[1024,768]{1,0:T(8,128)(2,1)S(1)} %get-tuple-element.24, bf16[1024,4096]{1,0:T(8,128)(2,1)} %bitcast.23), kind=kOutput, calls=%fused_computation.11 | convolution fusion | flops 3222798336 | bytes 8912896 | tf_op jit(solution)/shard_map/dot_general | solution.py:32
  145.7 0.0 copy-done.3
  145.8 0.0 slice-start.1
  145.8 7.6 %fusion.18 = bf16[1,2048,768]{2,1,0:T(8,128)(2,1)} fusion(bf16[1024,768]{1,0:T(8,128)(2,1)S(1)} %copy-done.3, bf16[1024,4096]{1,0:T(8,128)(2,1)} %bitcast.24), kind=kOutput, calls=%fused_computation.10 | convolution fusion | flops 3222798336 | bytes 8912896 | tf_op jit(solution)/shard_map/dot_general | solution.py:32
  153.3 0.0 slice-done
  153.3 0.0 slice-done.1
  153.3 4.8 %fusion.15 = bf16[1,768,2048]{2,1,0:T(8,128)(2,1)} fusion(bf16[1024,768]{1,0:T(8,128)(2,1)S(1)} %get-tuple-element.26, bf16[1024,4096]{1,0:T(8,128)(2,1)S(1)} %bitcast.27), kind=kOutput, calls=%fused_computation.9 | convolution fusion | flops 3222798336 | bytes 8912896 | tf_op jit(solution)/shard_map/dot_general | solution.py:32
  158.1 35.2 %all-to-all-done.1 = bf16[128,8,2176]{2,1,0:T(8,128)(2,1)} async-done(((bf16[128,8,2176]{2,1,0:T(8,128)(2,1)}), bf16[128,8,2176]{2,1,0:T(8,128)(2,1)}, u32[]{:S(2)}, u32[]{:S(2)}) %all-to-all-start.1) | async-done | bytes 4456480 | tf_op jit(solution)/shard_map/all_to_all | solution.py:230
  193.3 3.3 %collect_rows.1 = (bf16[64,2048]{1,0:T(8,128)(2,1)}, f32[64,128]{1,0:T(8,128)}) custom-call(bf16[64,1024]{1,0:T(8,128)(2,1)S(1)} %get-tuple-element.16.pick_ref, f32[64,128]{1,0:T(8,128)S(1)} %get-tuple-element.17.w_ref, f32[64,128]{1,0:T(8,128)S(1)} %get-tuple-element.18.sum_ref, bf16[1024,2176]{1,0:T(8,128)(2,1)} %bitcast.7.back_hbm), custom_call_target="tpu_custom_call" | custom-call | tf_op jit(solution)/shard_map/collect_rows/pallas_call | solution.py:212
  (1 shorter events, 0.0 us)
Async XLA Ops:
  4.4 108.8 %copy-start = (bf16[1,2048,768]{2,1,0:T(8,128)(2,1)S(1)}, bf16[1,2048,768]{2,1,0:T(8,128)(2,1)}, u32[]{:S(2)}) copy-start(bf16[1,2048,768]{2,1,0:T(8,128)(2,1)} %param.11) | copy-start | bytes 9437188
  4.4 108.8 %copy-start.1 = (bf16[1,2048,768]{2,1,0:T(8,128)(2,1)S(1)}, bf16[1,2048,768]{2,1,0:T(8,128)(2,1)}, u32[]{:S(2)}) copy-start(bf16[1,2048,768]{2,1,0:T(8,128)(2,1)} %param.12) | copy-start | bytes 9437188
  4.5 108.8 %copy-start.2 = (bf16[1,768,2048]{2,1,0:T(8,128)(2,1)S(1)}, bf16[1,768,2048]{2,1,0:T(8,128)(2,1)}, u32[]{:S(2)}) copy-start(bf16[1,768,2048]{2,1,0:T(8,128)(2,1)} %param.13) | copy-start | bytes 9437188
  133.1 60.2 %all-to-all-start.1 = ((bf16[128,8,2176]{2,1,0:T(8,128)(2,1)}), bf16[128,8,2176]{2,1,0:T(8,128)(2,1)}, u32[]{:S(2)}, u32[]{:S(2)}) async-start(bf16[128,8,2176]{2,1,0:T(8,128)(2,1)} %bitcast.28), calls=%async_computation.1 | async-start | bytes 8912896 | tf_op jit(solution)/shard_map/all_to_all | solution.py:230
  138.2 7.6 %copy-start.3 = (bf16[1024,768]{1,0:T(8,128)(2,1)S(1)}, bf16[1024,768]{1,0:T(8,128)(2,1)}, u32[]{:S(2)}) copy-start(bf16[1024,768]{1,0:T(8,128)(2,1)} %get-tuple-element.25) | copy-start | bytes 4718596
  138.2 15.1 %slice-start = ((s8[8388608]{0:T(1024)(128)(4,1)}), s8[4194304]{0:T(1024)(128)(4,1)S(1)}, s32[]{:S(2)}) async-start(s8[8388608]{0:T(1024)(128)(4,1)} %bitcast.25), calls=%async_computation.2 | async-start | bytes 8388608
  145.8 7.6 %slice-start.1 = ((s8[8388608]{0:T(1024)(128)(4,1)}), s8[4194304]{0:T(1024)(128)(4,1)S(1)}, s32[]{:S(2)}) async-start(s8[8388608]{0:T(1024)(128)(4,1)} %bitcast.25), calls=%async_computation.3 | async-start | bytes 8388608

commit v6 on v5

--- a/solution.py
+++ b/solution.py
@@ -81,9 +81,8 @@
     chosen = chosen.astype(bf16)
     copies[2].wait()
     copies[3].wait()
-    for at in range(0, width, 512):
-        x_ref[:, at : at + 512] = nn(chosen, tok_ref[:, at : at + 512]).astype(bf16)
-        x_ref[:, width + at : width + at + 512] = nn(weights, grad_ref[:, at : at + 512]).astype(bf16)
+    x_ref[:, :width] = nn(chosen, tok_ref[...]).astype(bf16)
+    x_ref[:, width:] = nn(weights, grad_ref[...]).astype(bf16)
 
 
 def send_rows(ids, probs, tokens, grads):
@@ -125,16 +124,16 @@
         terms += term[:, :LANES] + term[:, LANES:]
         dg_ref[:, part] = (back * up * sig * (1.0 + gate * (1.0 - sig))).astype(bf16)
         du_ref[:, part] = (back * silu).astype(bf16)
+    route = jnp.sum(terms, axis=1, keepdims=True)
+    high = route.astype(bf16).astype(f32)
+    turn = (iota((rows, LANES), 1) // (LANES // CAP) - iota((rows, LANES), 0) % CAP + CAP) % CAP
+    extra = jnp.where(turn == 4, high, jnp.where(turn == 5, route - high, cnt_ref[...]))
+    out_ref[:, width:] = extra.astype(bf16)
     d_gate = dg_ref[...]
     d_up = du_ref[...]
     for at in range(0, width, 512):
         cols = slice(at, at + 512)
         out_ref[:, cols] = (nt(d_gate, gate_ref[cols, :]) + nt(d_up, up_ref[cols, :])).astype(bf16)
-    route = jnp.sum(terms, axis=1, keepdims=True)
-    high = route.astype(bf16).astype(f32)
-    turn = (iota((rows, LANES), 1) // (LANES // CAP) - iota((rows, LANES), 0) % CAP + CAP) % CAP
-    extra = jnp.where(turn == 4, high, jnp.where(turn == 5, route - high, cnt_ref[...]))
-    out_ref[:, width:] = extra.astype(bf16)
 
 
 def expert_rows(x, gate, up, down, counts):

time: 197 us -> 197 us (level)
  no operation moved by 1% of the time
where the time goes in v6:
time: 197 us
  blocking collectives  109 us (55%)
  waiting for transfers between devices  35.2 us (18%)
  Pallas kernels  27 us (14%)
  matrix products  19.9 us (10%)
  starting transfers between devices  5.05 us (3%)
    all_to_all x1, blocking collectives, exchange(): lax.all_to_all(rows.reshape(devices, slots // devices, width), AXES, spli...  109 us
    all_to_all x1, waiting for transfers between devices, exchange(): lax.all_to_all(rows.reshape(devices, slots // devices, width), AXES, spli...  35.2 us
    dot_general x3, matrix products, tn(): lax.dot_general(left, right, (((0,), (0,)), ((), ())), preferred_element_...  19.9 us
    pallas_call x1, Pallas kernels, expert_rows(): pl.pallas_call(expert_kernel, grid=(slots // rows,), in_specs=[block(widt...  19.8 us
    all_to_all x1, starting transfers between devices, exchange(): lax.all_to_all(rows.reshape(devices, slots // devices, width), AXES, spli...  5.05 us
  transfers between devices with their start and end apart: 1, of which 1 were waited for; matrix products, arithmetic and copies ran while one was open for 10% of the time, Pallas kernels for 0%

profile of v6, /device:TPU:1, one launch (start us, length us, event | category | flops | bytes accessed | tf_op | source)
XLA Modules:
  0.0 196.8 jit_solution(14986556652621844800)
XLA Ops:
  0.6 3.8 %send_rows.1 = (bf16[1024,4096]{1,0:T(8,128)(2,1)S(1)}, bf16[64,1024]{1,0:T(8,128)(2,1)S(1)}, f32[64,128]{1,0:T(8,128)S(1)}, f32[64,128]{1,0:T(8,128)S(1)}, f32[256,128]{1,0:T(8,128)S(1)}) custom-call(s32[8,64]{1,0:T(8,128)} %bitcast.29, f32[64,128]{1,0:T(8,128)} %probs_hbm.1, bf16[64,2048]{1,0:T(8,128)(2,1)} %tok_hbm.1, bf16[64,2048]{1,0:T(8,128)(2,1)} %grad_hbm.1), custom_call_target="tpu_custom_call" | custom-call | tf_op jit(solution)/shard_map/send_rows/pallas_call | solution.py:93
  4.4 0.0 copy-start
  4.4 0.0 copy-start.1
  4.5 0.0 copy-start.2
  4.5 108.8 %all_to_all.10 = bf16[128,8,4096]{2,1,0:T(8,128)(2,1)} all-to-all(bf16[128,8,4096]{2,1,0:T(8,128)(2,1)S(1)} %bitcast.17), channel_id=1, replica_groups=mesh['dp'=8,'expert'=16] {'dp','expert'}, dimensions={0} | all-to-all | bytes 16777216 | tf_op jit(solution)/shard_map/all_to_all | solution.py:229
  113.3 0.0 copy-done
  113.3 0.0 copy-done.1
  113.3 0.0 copy-done.2
  113.3 19.8 %expert_rows.1 = (bf16[1024,2176]{1,0:T(8,128)(2,1)}, bf16[1024,768]{1,0:T(8,128)(2,1)S(1)}, bf16[1024,768]{1,0:T(8,128)(2,1)S(1)}, bf16[1024,768]{1,0:T(8,128)(2,1)}) custom-call(bf16[1024,4096]{1,0:T(8,128)(2,1)} %bitcast.21, bf16[1024,4096]{1,0:T(8,128)(2,1)} %bitcast.22, bf16[2048,768]{1,0:T(8,128)(2,1)S(1)} %bitcast.18, bf16[2048,768]{1,0:T(8,128)(2,1)S(1)} %bitcast.19, ...), custom_call_target="tpu_custom_call" | custom-call | tf_op jit(solution)/shard_map/expert_rows/pallas_call | solution.py:146
  133.1 5.0 %all-to-all-start.1 = ((bf16[128,8,2176]{2,1,0:T(8,128)(2,1)}), bf16[128,8,2176]{2,1,0:T(8,128)(2,1)}, u32[]{:S(2)}, u32[]{:S(2)}) async-start(bf16[128,8,2176]{2,1,0:T(8,128)(2,1)} %bitcast.28), calls=%async_computation.1 | async-start | bytes 8912896 | tf_op jit(solution)/shard_map/all_to_all | solution.py:229
  138.2 0.0 copy-start.3
  138.2 0.0 slice-start
  138.2 7.5 %fusion.21 = bf16[1,2048,768]{2,1,0:T(8,128)(2,1)} fusion(bf16[1024,768]{1,0:T(8,128)(2,1)S(1)} %get-tuple-element.24, bf16[1024,4096]{1,0:T(8,128)(2,1)} %bitcast.23), kind=kOutput, calls=%fused_computation.11 | convolution fusion | flops 3222798336 | bytes 8912896 | tf_op jit(solution)/shard_map/dot_general | solution.py:32
  145.7 0.0 copy-done.3
  145.7 0.0 slice-start.1
  145.8 7.6 %fusion.18 = bf16[1,2048,768]{2,1,0:T(8,128)(2,1)} fusion(bf16[1024,768]{1,0:T(8,128)(2,1)S(1)} %copy-done.3, bf16[1024,4096]{1,0:T(8,128)(2,1)} %bitcast.24), kind=kOutput, calls=%fused_computation.10 | convolution fusion | flops 3222798336 | bytes 8912896 | tf_op jit(solution)/shard_map/dot_general | solution.py:32
  153.3 0.0 slice-done
  153.3 0.0 slice-done.1
  153.3 4.8 %fusion.15 = bf16[1,768,2048]{2,1,0:T(8,128)(2,1)} fusion(bf16[1024,768]{1,0:T(8,128)(2,1)S(1)} %get-tuple-element.26, bf16[1024,4096]{1,0:T(8,128)(2,1)S(1)} %bitcast.27), kind=kOutput, calls=%fused_computation.9 | convolution fusion | flops 3222798336 | bytes 8912896 | tf_op jit(solution)/shard_map/dot_general | solution.py:32
  158.1 35.2 %all-to-all-done.1 = bf16[128,8,2176]{2,1,0:T(8,128)(2,1)} async-done(((bf16[128,8,2176]{2,1,0:T(8,128)(2,1)}), bf16[128,8,2176]{2,1,0:T(8,128)(2,1)}, u32[]{:S(2)}, u32[]{:S(2)}) %all-to-all-start.1) | async-done | bytes 4456480 | tf_op jit(solution)/shard_map/all_to_all | solution.py:229
  193.3 3.3 %collect_rows.1 = (bf16[64,2048]{1,0:T(8,128)(2,1)}, f32[64,128]{1,0:T(8,128)}) custom-call(bf16[64,1024]{1,0:T(8,128)(2,1)S(1)} %get-tuple-element.16.pick_ref, f32[64,128]{1,0:T(8,128)S(1)} %get-tuple-element.17.w_ref, f32[64,128]{1,0:T(8,128)S(1)} %get-tuple-element.18.sum_ref, bf16[1024,2176]{1,0:T(8,128)(2,1)} %bitcast.7.back_hbm), custom_call_target="tpu_custom_call" | custom-call | tf_op jit(solution)/shard_map/collect_rows/pallas_call | solution.py:211
  (1 shorter events, 0.0 us)
Async XLA Ops:
  4.4 108.8 %copy-start = (bf16[1,2048,768]{2,1,0:T(8,128)(2,1)S(1)}, bf16[1,2048,768]{2,1,0:T(8,128)(2,1)}, u32[]{:S(2)}) copy-start(bf16[1,2048,768]{2,1,0:T(8,128)(2,1)} %param.11) | copy-start | bytes 9437188
  4.4 108.8 %copy-start.1 = (bf16[1,2048,768]{2,1,0:T(8,128)(2,1)S(1)}, bf16[1,2048,768]{2,1,0:T(8,128)(2,1)}, u32[]{:S(2)}) copy-start(bf16[1,2048,768]{2,1,0:T(8,128)(2,1)} %param.12) | copy-start | bytes 9437188
  4.5 108.8 %copy-start.2 = (bf16[1,768,2048]{2,1,0:T(8,128)(2,1)S(1)}, bf16[1,768,2048]{2,1,0:T(8,128)(2,1)}, u32[]{:S(2)}) copy-start(bf16[1,768,2048]{2,1,0:T(8,128)(2,1)} %param.13) | copy-start | bytes 9437188
  133.1 60.2 %all-to-all-start.1 = ((bf16[128,8,2176]{2,1,0:T(8,128)(2,1)}), bf16[128,8,2176]{2,1,0:T(8,128)(2,1)}, u32[]{:S(2)}, u32[]{:S(2)}) async-start(bf16[128,8,2176]{2,1,0:T(8,128)(2,1)} %bitcast.28), calls=%async_computation.1 | async-start | bytes 8912896 | tf_op jit(solution)/shard_map/all_to_all | solution.py:229
  138.2 7.6 %copy-start.3 = (bf16[1024,768]{1,0:T(8,128)(2,1)S(1)}, bf16[1024,768]{1,0:T(8,128)(2,1)}, u32[]{:S(2)}) copy-start(bf16[1024,768]{1,0:T(8,128)(2,1)} %get-tuple-element.25) | copy-start | bytes 4718596
  138.2 15.1 %slice-start = ((s8[8388608]{0:T(1024)(128)(4,1)}), s8[4194304]{0:T(1024)(128)(4,1)S(1)}, s32[]{:S(2)}) async-start(s8[8388608]{0:T(1024)(128)(4,1)} %bitcast.25), calls=%async_computation.2 | async-start | bytes 8388608
  145.7 7.6 %slice-start.1 = ((s8[8388608]{0:T(1024)(128)(4,1)}), s8[4194304]{0:T(1024)(128)(4,1)S(1)}, s32[]{:S(2)}) async-start(s8[8388608]{0:T(1024)(128)(4,1)} %bitcast.25), calls=%async_computation.3 | async-start | bytes 8388608
